TPU v7x, 32 devices: a whole 2x2x4 slice. The times are simulated.
32 devices in a mesh: proj: 8 (over z, x), lang: 4 (over y, core).
Axes of the slice: x: 2, y: 2, z: 4, core: 2. Of those that a mesh axis runs over, the one named last changes fastest.
Arguments:
- mapped_layer_arguments: bfloat16 [48, 512, 8192], P('lang', None, 'proj'), may hold values from -6 to 6
- loss_slope_at_result: bfloat16 [48, 512, 8192], P('lang', None, 'proj'), may hold values from -6 to 6
- left_lowrank_weights: bfloat16 [8192, 128], P('proj'), may hold values from -0.0625 to 0.0625
- right_lowrank_weights: bfloat16 [128, 8192], P(None, 'proj'), may hold values from -0.0625 to 0.0625
- mean_estimate_left: float32 [8192, 128], P('proj'), may hold values from -24 to 24
- variance_estimate_left: float32 [8192, 128], P('proj'), may hold values from 0.1 to 10
- mean_estimate_right: float32 [128, 8192], P(None, 'proj'), may hold values from -24 to 24
- variance_estimate_right: float32 [128, 8192], P(None, 'proj'), may hold values from 0.1 to 10
- heldout_sketched_slopes: bfloat16 [8, 256, 8192], P('lang', None, 'proj'), may hold values from -600 to 600
- tongue_label_per_example: int32 [48, 1], P('lang'), may hold values from 0 to 7; in each aligned block of 12 rows (0 to 11, 12 to 23, ...) at most 3 rows name the same one
- heldout_example_tally: int32 [8], replicated, may hold values from 1 to 256, 1280 in all
- sketch_random_key: int32 [1], replicated, may hold values from 0 to 16777215
Outputs:
- features: float32 [48, 8192], P('lang', 'proj')
- scores: float32 [48], P('lang')
Inputs may be any that keep to these rules, and one draw needn't show every extreme that they name: `tongue_label_per_example`: among the 12 samples of one device, in aligned blocks of rows, no language appears more than 3 times.
All inputs are finite; a program needn't handle non-finite values.
Results may differ from a plain program's by a relative error of at most 0.0049.
Values may be sent and summed in bfloat16 or wider, within the bound.
A program may use at most 128 MiB of HBM per device.

v0:
```python
import math

import jax
import jax.numpy as jnp
from jax import lax
from jax.sharding import PartitionSpec as P

LOWRANK_INNER = 128
K = 8192
NVAL = 256


update_multiplier = 1.25


def scramble(hashed):
    hashed = jnp.bitwise_xor(hashed, lax.shift_right_logical(hashed, jnp.int32(16)))
    hashed = hashed * 2146121005
    hashed = jnp.bitwise_xor(hashed, lax.shift_right_logical(hashed, jnp.int32(15)))
    hashed = hashed * 739982445
    hashed = jnp.bitwise_xor(hashed, lax.shift_right_logical(hashed, jnp.int32(16)))
    return hashed


def sign_table(seed_value, table_id, row_count, row_start, col_count):
    row_ids = row_start + lax.iota(jnp.int32, row_count)
    col_ids = lax.iota(jnp.int32, col_count)
    anchor = scramble(seed_value * 4 + table_id)
    hashed = scramble(anchor + row_ids[:, None] * col_count + col_ids[None, :])
    sign_bit = jnp.bitwise_and(lax.shift_right_logical(hashed, jnp.int32(13)), 1)
    return (1 - 2 * sign_bit).astype(jnp.float32)


def precondition(gradient, moment, second):
    return (
        (0.9 * moment + 0.1 * gradient) * lax.rsqrt(0.999 * second + 0.001 * gradient * gradient)
    ).astype(jnp.bfloat16)


def per_device(
    mapped_layer_arguments,
    loss_slope_at_result,
    left_lowrank_weights,
    right_lowrank_weights,
    mean_estimate_left,
    variance_estimate_left,
    mean_estimate_right,
    variance_estimate_right,
    heldout_sketched_slopes,
    tongue_label_per_example,
    heldout_example_tally,
    sketch_random_key,
):
    shard_id = lax.axis_index("proj")
    width_dev = mapped_layer_arguments.shape[2]
    seed_value = sketch_random_key[0]
    row_start = shard_id * width_dev
    anchor_row = jnp.int32(0)
    up_left = sign_table(seed_value, 0, LOWRANK_INNER, anchor_row, K).astype(jnp.bfloat16)
    up_right = sign_table(seed_value, 1, width_dev, row_start, K).astype(jnp.bfloat16)
    down_left = sign_table(seed_value, 2, width_dev, row_start, K).astype(jnp.bfloat16)
    down_right = sign_table(seed_value, 3, LOWRANK_INNER, anchor_row, K).astype(jnp.bfloat16)

    def sample_terms(
        entering_signal_accumulated,
        output_slope_accumulated,
        entering_signals,
        output_slope_gathered,
    ):
        grad_up = jnp.einsum(
            "tr,tc->rc",
            entering_signal_accumulated,
            output_slope_gathered,
            preferred_element_type=jnp.float32,
        )
        grad_down = jnp.einsum(
            "tc,tr->cr",
            entering_signals,
            output_slope_accumulated,
            preferred_element_type=jnp.float32,
        )
        step_up = precondition(grad_up, mean_estimate_right, variance_estimate_right)
        step_down = precondition(grad_down, mean_estimate_left, variance_estimate_left)
        mixed_up = jnp.dot(step_up, up_right, preferred_element_type=jnp.float32)
        mixed_down = jnp.einsum(
            "cr,ck->rk", step_down, down_left, preferred_element_type=jnp.float32
        )
        return jnp.sum(mixed_up * up_left + mixed_down * down_right, axis=0)

    partial_input = jnp.einsum(
        "wqz,zk->wqk",
        mapped_layer_arguments,
        left_lowrank_weights,
        preferred_element_type=jnp.float32,
    )
    partial_gradient = jnp.einsum(
        "jkh,wh->jkw",
        loss_slope_at_result,
        right_lowrank_weights,
        preferred_element_type=jnp.float32,
    )
    input_summed_rows, gradient_summed_rows = lax.psum((partial_input, partial_gradient), "proj")
    entering_signal_accumulated = (update_multiplier * input_summed_rows).astype(jnp.bfloat16)
    output_slope_accumulated = (update_multiplier * gradient_summed_rows).astype(jnp.bfloat16)

    def whole_sample(sample_item):
        return sample_terms(sample_item[0], sample_item[1], sample_item[2], sample_item[3])

    projected = lax.map(
        whole_sample,
        (
            entering_signal_accumulated,
            output_slope_accumulated,
            mapped_layer_arguments,
            loss_slope_at_result,
        ),
    )
    share_width = K // lax.axis_size("proj")
    summed = lax.psum(projected, "proj")
    full_rows = summed * lax.rsqrt(jnp.mean(summed * summed, axis=-1, keepdims=True) + 1e-06)
    features = lax.dynamic_slice_in_dim(full_rows, shard_id * share_width, share_width, 1)
    feat_low = features.astype(jnp.bfloat16)
    lang_of = tongue_label_per_example[:, 0]
    num_langs = heldout_example_tally.shape[0]
    one_hot = (lang_of[:, None] == lax.iota(jnp.int32, num_langs)[None, :]).astype(jnp.int32)
    root_scale = math.sqrt(K)
    all_val = lax.all_gather(heldout_sketched_slopes, "lang", axis=0, tiled=True)
    partial_all = jnp.einsum("nc,ljc->nlj", feat_low, all_val, preferred_element_type=jnp.float32)
    own_part = jnp.sum(partial_all * one_hot[:, :, None].astype(jnp.float32), axis=1)
    val_wide = all_val.astype(jnp.float32)
    partial_sq = jnp.sum(val_wide * val_wide, axis=-1)
    dot_sums, val_square = lax.psum((own_part, partial_sq), "proj")
    rms_all = jnp.sqrt(val_square / K + 1e-06)
    rms_own = jnp.sum(one_hot[:, :, None].astype(jnp.float32) * rms_all[None, :, :], axis=1)
    count_own = jnp.sum(one_hot * heldout_example_tally[None, :], axis=1)
    similar = dot_sums / (root_scale * rms_own)
    is_valid = lax.iota(jnp.int32, NVAL)[None, :] < count_own[:, None]
    scores = jnp.max(jnp.where(is_valid, similar, jnp.float32(-1e30)), axis=-1)
    return (features, scores)


def solution(mesh):
    in_specs = (
        P("lang", None, "proj"),
        P("lang", None, "proj"),
        P("proj", None),
        P(None, "proj"),
        P("proj", None),
        P("proj", None),
        P(None, "proj"),
        P(None, "proj"),
        P("lang", None, "proj"),
        P("lang", None),
        P(),
        P(),
    )
    out_specs = (P("lang", "proj"), P("lang"))
    return jax.shard_map(
        per_device, mesh=mesh, in_specs=in_specs, out_specs=out_specs, check_vma=False
    )
```

profile of v0, /device:TPU:0, one launch (start us, length us, event | category | flops | bytes accessed | tf_op | source)
XLA Modules:
  0.0 985.0 jit_solution(1025482407241696007)
XLA Ops:
  8.0 0.0 copy-start
  8.0 0.0 all-reduce.7.cloned.1.call-start
  8.1 0.9 copy-done
  9.0 9.8 fusion.123
  18.8 0.0 copy-done.1
  18.8 5.3 fusion.125
  24.1 0.0 all-reduce.7.cloned.1.call-update
  24.1 0.0 all-gather.2.cloned.1.call-start
  24.2 0.5 all-gather.2.cloned.1.call-update
  24.7 0.0 all-reduce.5.cloned.1.call-start
  25.5 0.6 convert_convert_fusion
  26.1 213.3 %all-reduce.7.cloned.1.call-done = (f32[12,512,128]{2,1,0:T(8,128)}, f32[12,512,128]{2,1,0:T(8,128)}) async-done(((f32[12,512,128]{2,1,0:T(8,128)}, f32[12,512,128]{2,1,0:T(8,128)}), (f32[12,512,128]{2,1,0:T(8,128)}, f32[12,512,128]{2,1,0:T(8,128)})) %all-reduce.7.cloned.1.call-update) | async-done | bytes 6291472 | tf_op jit(solution)/shard_map/psum | solution.py:102
  239.4 3.6 multiply_convert_fusion
  243.0 0.0 copy-start.6
  243.0 0.0 copy-start.7
  243.0 621.1 %while.11 = (s32[]{:T(128)}, f32[12,8192]{1,0:T(8,128)}, f32[128,1024]{1,0:T(8,128)}, bf16[12,512,128]{2,1,0:T(8,128)(2,1)S(1)}, bf16[12,512,1024]{2,1,0:T(8,128...) while((s32[]{:T(128)}, f32[12,8192]{1,0:T(8,128)}, ...), condition=%wide.region_4.5_spmd.clone, body=%wide.region_2.4_spmd.clone.sunk | while | flops 4855160832 | bytes 12954777 | solution.py:109
  243.4 24.4 %fusion.150 = f32[128,8192]{1,0:T(8,128)} fusion(s32[1024]{0:T(1024)S(1)} %get-tuple-element.279, s32[128]{0:T(128)S(1)} %get-tuple-element.280, f32[1024,128]{1,0:T(8,128)} %get-tuple-element.276, bf16[12,512,1024]{2,1,0:T(8,128)(2,1)} %get-tuple-element.274, s32[]{:T(128)} %get-tuple-element.251, f32[1024,128]{1,0:T(8,128)} %get-tuple-element.273, ...), kind=kOutput, calls=%fused_computation.30.clone.1 | convolution fusion | flops 2426535936 | bytes 6428160 | tf_op jit(solution)/shard_map/while/body/eval_jaxpr/cr,ck->rk/dot_general | solution.py:85
  267.8 23.8 %fusion.151 = f32[8192]{0:T(1024)S(1)} fusion(f32[128,8192]{1,0:T(8,128)} %fusion.150, s32[128]{0:T(128)S(1)} %get-tuple-element.278, s32[1024]{0:T(1024)S(1)} %get-tuple-element.277, f32[128,1024]{1,0:T(8,128)} %get-tuple-element.272, bf16[12,512,1024]{2,1,0:T(8,128)(2,1)} %get-tuple-element.271, s32[]{:T(128)} %get-tuple-element.251, ...), kind=kOutput, calls=%fused_computation.53.clone.1 | convolution fusion | flops 2428624896 | bytes 6460928 | tf_op jit(solution)/shard_map/while/body/eval_jaxpr/dot_general | solution.py:84
  291.6 1.8 dynamic_update_slice.6
  295.1 24.1 %fusion.150 = f32[128,8192]{1,0:T(8,128)} fusion(s32[1024]{0:T(1024)S(1)} %get-tuple-element.279, s32[128]{0:T(128)S(1)} %get-tuple-element.280, f32[1024,128]{1,0:T(8,128)} %get-tuple-element.276, bf16[12,512,1024]{2,1,0:T(8,128)(2,1)} %get-tuple-element.274, s32[]{:T(128)} %get-tuple-element.251, f32[1024,128]{1,0:T(8,128)} %get-tuple-element.273, ...), kind=kOutput, calls=%fused_computation.30.clone.1 | convolution fusion | flops 2426535936 | bytes 6428160 | tf_op jit(solution)/shard_map/while/body/eval_jaxpr/cr,ck->rk/dot_general | solution.py:85
  319.2 24.1 %fusion.151 = f32[8192]{0:T(1024)S(1)} fusion(f32[128,8192]{1,0:T(8,128)} %fusion.150, s32[128]{0:T(128)S(1)} %get-tuple-element.278, s32[1024]{0:T(1024)S(1)} %get-tuple-element.277, f32[128,1024]{1,0:T(8,128)} %get-tuple-element.272, bf16[12,512,1024]{2,1,0:T(8,128)(2,1)} %get-tuple-element.271, s32[]{:T(128)} %get-tuple-element.251, ...), kind=kOutput, calls=%fused_computation.53.clone.1 | convolution fusion | flops 2428624896 | bytes 6460928 | tf_op jit(solution)/shard_map/while/body/eval_jaxpr/dot_general | solution.py:84
  343.3 1.8 dynamic_update_slice.6
  346.5 24.2 %fusion.150 = f32[128,8192]{1,0:T(8,128)} fusion(s32[1024]{0:T(1024)S(1)} %get-tuple-element.279, s32[128]{0:T(128)S(1)} %get-tuple-element.280, f32[1024,128]{1,0:T(8,128)} %get-tuple-element.276, bf16[12,512,1024]{2,1,0:T(8,128)(2,1)} %get-tuple-element.274, s32[]{:T(128)} %get-tuple-element.251, f32[1024,128]{1,0:T(8,128)} %get-tuple-element.273, ...), kind=kOutput, calls=%fused_computation.30.clone.1 | convolution fusion | flops 2426535936 | bytes 6428160 | tf_op jit(solution)/shard_map/while/body/eval_jaxpr/cr,ck->rk/dot_general | solution.py:85
  370.6 24.0 %fusion.151 = f32[8192]{0:T(1024)S(1)} fusion(f32[128,8192]{1,0:T(8,128)} %fusion.150, s32[128]{0:T(128)S(1)} %get-tuple-element.278, s32[1024]{0:T(1024)S(1)} %get-tuple-element.277, f32[128,1024]{1,0:T(8,128)} %get-tuple-element.272, bf16[12,512,1024]{2,1,0:T(8,128)(2,1)} %get-tuple-element.271, s32[]{:T(128)} %get-tuple-element.251, ...), kind=kOutput, calls=%fused_computation.53.clone.1 | convolution fusion | flops 2428624896 | bytes 6460928 | tf_op jit(solution)/shard_map/while/body/eval_jaxpr/dot_general | solution.py:84
  394.7 1.8 dynamic_update_slice.6
  398.0 24.4 %fusion.150 = f32[128,8192]{1,0:T(8,128)} fusion(s32[1024]{0:T(1024)S(1)} %get-tuple-element.279, s32[128]{0:T(128)S(1)} %get-tuple-element.280, f32[1024,128]{1,0:T(8,128)} %get-tuple-element.276, bf16[12,512,1024]{2,1,0:T(8,128)(2,1)} %get-tuple-element.274, s32[]{:T(128)} %get-tuple-element.251, f32[1024,128]{1,0:T(8,128)} %get-tuple-element.273, ...), kind=kOutput, calls=%fused_computation.30.clone.1 | convolution fusion | flops 2426535936 | bytes 6428160 | tf_op jit(solution)/shard_map/while/body/eval_jaxpr/cr,ck->rk/dot_general | solution.py:85
  422.3 23.8 %fusion.151 = f32[8192]{0:T(1024)S(1)} fusion(f32[128,8192]{1,0:T(8,128)} %fusion.150, s32[128]{0:T(128)S(1)} %get-tuple-element.278, s32[1024]{0:T(1024)S(1)} %get-tuple-element.277, f32[128,1024]{1,0:T(8,128)} %get-tuple-element.272, bf16[12,512,1024]{2,1,0:T(8,128)(2,1)} %get-tuple-element.271, s32[]{:T(128)} %get-tuple-element.251, ...), kind=kOutput, calls=%fused_computation.53.clone.1 | convolution fusion | flops 2428624896 | bytes 6460928 | tf_op jit(solution)/shard_map/while/body/eval_jaxpr/dot_general | solution.py:84
  446.2 1.8 dynamic_update_slice.6
  449.6 24.1 %fusion.150 = f32[128,8192]{1,0:T(8,128)} fusion(s32[1024]{0:T(1024)S(1)} %get-tuple-element.279, s32[128]{0:T(128)S(1)} %get-tuple-element.280, f32[1024,128]{1,0:T(8,128)} %get-tuple-element.276, bf16[12,512,1024]{2,1,0:T(8,128)(2,1)} %get-tuple-element.274, s32[]{:T(128)} %get-tuple-element.251, f32[1024,128]{1,0:T(8,128)} %get-tuple-element.273, ...), kind=kOutput, calls=%fused_computation.30.clone.1 | convolution fusion | flops 2426535936 | bytes 6428160 | tf_op jit(solution)/shard_map/while/body/eval_jaxpr/cr,ck->rk/dot_general | solution.py:85
  473.7 24.1 %fusion.151 = f32[8192]{0:T(1024)S(1)} fusion(f32[128,8192]{1,0:T(8,128)} %fusion.150, s32[128]{0:T(128)S(1)} %get-tuple-element.278, s32[1024]{0:T(1024)S(1)} %get-tuple-element.277, f32[128,1024]{1,0:T(8,128)} %get-tuple-element.272, bf16[12,512,1024]{2,1,0:T(8,128)(2,1)} %get-tuple-element.271, s32[]{:T(128)} %get-tuple-element.251, ...), kind=kOutput, calls=%fused_computation.53.clone.1 | convolution fusion | flops 2428624896 | bytes 6460928 | tf_op jit(solution)/shard_map/while/body/eval_jaxpr/dot_general | solution.py:84
  497.8 1.8 dynamic_update_slice.6
  501.0 24.2 %fusion.150 = f32[128,8192]{1,0:T(8,128)} fusion(s32[1024]{0:T(1024)S(1)} %get-tuple-element.279, s32[128]{0:T(128)S(1)} %get-tuple-element.280, f32[1024,128]{1,0:T(8,128)} %get-tuple-element.276, bf16[12,512,1024]{2,1,0:T(8,128)(2,1)} %get-tuple-element.274, s32[]{:T(128)} %get-tuple-element.251, f32[1024,128]{1,0:T(8,128)} %get-tuple-element.273, ...), kind=kOutput, calls=%fused_computation.30.clone.1 | convolution fusion | flops 2426535936 | bytes 6428160 | tf_op jit(solution)/shard_map/while/body/eval_jaxpr/cr,ck->rk/dot_general | solution.py:85
  525.2 24.0 %fusion.151 = f32[8192]{0:T(1024)S(1)} fusion(f32[128,8192]{1,0:T(8,128)} %fusion.150, s32[128]{0:T(128)S(1)} %get-tuple-element.278, s32[1024]{0:T(1024)S(1)} %get-tuple-element.277, f32[128,1024]{1,0:T(8,128)} %get-tuple-element.272, bf16[12,512,1024]{2,1,0:T(8,128)(2,1)} %get-tuple-element.271, s32[]{:T(128)} %get-tuple-element.251, ...), kind=kOutput, calls=%fused_computation.53.clone.1 | convolution fusion | flops 2428624896 | bytes 6460928 | tf_op jit(solution)/shard_map/while/body/eval_jaxpr/dot_general | solution.py:84
  549.3 1.8 dynamic_update_slice.6
  552.5 24.4 %fusion.150 = f32[128,8192]{1,0:T(8,128)} fusion(s32[1024]{0:T(1024)S(1)} %get-tuple-element.279, s32[128]{0:T(128)S(1)} %get-tuple-element.280, f32[1024,128]{1,0:T(8,128)} %get-tuple-element.276, bf16[12,512,1024]{2,1,0:T(8,128)(2,1)} %get-tuple-element.274, s32[]{:T(128)} %get-tuple-element.251, f32[1024,128]{1,0:T(8,128)} %get-tuple-element.273, ...), kind=kOutput, calls=%fused_computation.30.clone.1 | convolution fusion | flops 2426535936 | bytes 6428160 | tf_op jit(solution)/shard_map/while/body/eval_jaxpr/cr,ck->rk/dot_general | solution.py:85
  576.9 23.8 %fusion.151 = f32[8192]{0:T(1024)S(1)} fusion(f32[128,8192]{1,0:T(8,128)} %fusion.150, s32[128]{0:T(128)S(1)} %get-tuple-element.278, s32[1024]{0:T(1024)S(1)} %get-tuple-element.277, f32[128,1024]{1,0:T(8,128)} %get-tuple-element.272, bf16[12,512,1024]{2,1,0:T(8,128)(2,1)} %get-tuple-element.271, s32[]{:T(128)} %get-tuple-element.251, ...), kind=kOutput, calls=%fused_computation.53.clone.1 | convolution fusion | flops 2428624896 | bytes 6460928 | tf_op jit(solution)/shard_map/while/body/eval_jaxpr/dot_general | solution.py:84
  600.7 1.8 dynamic_update_slice.6
  604.2 24.1 %fusion.150 = f32[128,8192]{1,0:T(8,128)} fusion(s32[1024]{0:T(1024)S(1)} %get-tuple-element.279, s32[128]{0:T(128)S(1)} %get-tuple-element.280, f32[1024,128]{1,0:T(8,128)} %get-tuple-element.276, bf16[12,512,1024]{2,1,0:T(8,128)(2,1)} %get-tuple-element.274, s32[]{:T(128)} %get-tuple-element.251, f32[1024,128]{1,0:T(8,128)} %get-tuple-element.273, ...), kind=kOutput, calls=%fused_computation.30.clone.1 | convolution fusion | flops 2426535936 | bytes 6428160 | tf_op jit(solution)/shard_map/while/body/eval_jaxpr/cr,ck->rk/dot_general | solution.py:85
  628.3 24.1 %fusion.151 = f32[8192]{0:T(1024)S(1)} fusion(f32[128,8192]{1,0:T(8,128)} %fusion.150, s32[128]{0:T(128)S(1)} %get-tuple-element.278, s32[1024]{0:T(1024)S(1)} %get-tuple-element.277, f32[128,1024]{1,0:T(8,128)} %get-tuple-element.272, bf16[12,512,1024]{2,1,0:T(8,128)(2,1)} %get-tuple-element.271, s32[]{:T(128)} %get-tuple-element.251, ...), kind=kOutput, calls=%fused_computation.53.clone.1 | convolution fusion | flops 2428624896 | bytes 6460928 | tf_op jit(solution)/shard_map/while/body/eval_jaxpr/dot_general | solution.py:84
  652.4 1.8 dynamic_update_slice.6
  655.6 24.2 %fusion.150 = f32[128,8192]{1,0:T(8,128)} fusion(s32[1024]{0:T(1024)S(1)} %get-tuple-element.279, s32[128]{0:T(128)S(1)} %get-tuple-element.280, f32[1024,128]{1,0:T(8,128)} %get-tuple-element.276, bf16[12,512,1024]{2,1,0:T(8,128)(2,1)} %get-tuple-element.274, s32[]{:T(128)} %get-tuple-element.251, f32[1024,128]{1,0:T(8,128)} %get-tuple-element.273, ...), kind=kOutput, calls=%fused_computation.30.clone.1 | convolution fusion | flops 2426535936 | bytes 6428160 | tf_op jit(solution)/shard_map/while/body/eval_jaxpr/cr,ck->rk/dot_general | solution.py:85
  679.8 24.0 %fusion.151 = f32[8192]{0:T(1024)S(1)} fusion(f32[128,8192]{1,0:T(8,128)} %fusion.150, s32[128]{0:T(128)S(1)} %get-tuple-element.278, s32[1024]{0:T(1024)S(1)} %get-tuple-element.277, f32[128,1024]{1,0:T(8,128)} %get-tuple-element.272, bf16[12,512,1024]{2,1,0:T(8,128)(2,1)} %get-tuple-element.271, s32[]{:T(128)} %get-tuple-element.251, ...), kind=kOutput, calls=%fused_computation.53.clone.1 | convolution fusion | flops 2428624896 | bytes 6460928 | tf_op jit(solution)/shard_map/while/body/eval_jaxpr/dot_general | solution.py:84
  703.8 1.8 dynamic_update_slice.6
  707.1 24.4 %fusion.150 = f32[128,8192]{1,0:T(8,128)} fusion(s32[1024]{0:T(1024)S(1)} %get-tuple-element.279, s32[128]{0:T(128)S(1)} %get-tuple-element.280, f32[1024,128]{1,0:T(8,128)} %get-tuple-element.276, bf16[12,512,1024]{2,1,0:T(8,128)(2,1)} %get-tuple-element.274, s32[]{:T(128)} %get-tuple-element.251, f32[1024,128]{1,0:T(8,128)} %get-tuple-element.273, ...), kind=kOutput, calls=%fused_computation.30.clone.1 | convolution fusion | flops 2426535936 | bytes 6428160 | tf_op jit(solution)/shard_map/while/body/eval_jaxpr/cr,ck->rk/dot_general | solution.py:85
  731.4 23.8 %fusion.151 = f32[8192]{0:T(1024)S(1)} fusion(f32[128,8192]{1,0:T(8,128)} %fusion.150, s32[128]{0:T(128)S(1)} %get-tuple-element.278, s32[1024]{0:T(1024)S(1)} %get-tuple-element.277, f32[128,1024]{1,0:T(8,128)} %get-tuple-element.272, bf16[12,512,1024]{2,1,0:T(8,128)(2,1)} %get-tuple-element.271, s32[]{:T(128)} %get-tuple-element.251, ...), kind=kOutput, calls=%fused_computation.53.clone.1 | convolution fusion | flops 2428624896 | bytes 6460928 | tf_op jit(solution)/shard_map/while/body/eval_jaxpr/dot_general | solution.py:84
  755.3 1.8 dynamic_update_slice.6
  758.7 24.1 %fusion.150 = f32[128,8192]{1,0:T(8,128)} fusion(s32[1024]{0:T(1024)S(1)} %get-tuple-element.279, s32[128]{0:T(128)S(1)} %get-tuple-element.280, f32[1024,128]{1,0:T(8,128)} %get-tuple-element.276, bf16[12,512,1024]{2,1,0:T(8,128)(2,1)} %get-tuple-element.274, s32[]{:T(128)} %get-tuple-element.251, f32[1024,128]{1,0:T(8,128)} %get-tuple-element.273, ...), kind=kOutput, calls=%fused_computation.30.clone.1 | convolution fusion | flops 2426535936 | bytes 6428160 | tf_op jit(solution)/shard_map/while/body/eval_jaxpr/cr,ck->rk/dot_general | solution.py:85
  782.9 24.1 %fusion.151 = f32[8192]{0:T(1024)S(1)} fusion(f32[128,8192]{1,0:T(8,128)} %fusion.150, s32[128]{0:T(128)S(1)} %get-tuple-element.278, s32[1024]{0:T(1024)S(1)} %get-tuple-element.277, f32[128,1024]{1,0:T(8,128)} %get-tuple-element.272, bf16[12,512,1024]{2,1,0:T(8,128)(2,1)} %get-tuple-element.271, s32[]{:T(128)} %get-tuple-element.251, ...), kind=kOutput, calls=%fused_computation.53.clone.1 | convolution fusion | flops 2428624896 | bytes 6460928 | tf_op jit(solution)/shard_map/while/body/eval_jaxpr/dot_general | solution.py:84
  806.9 1.8 dynamic_update_slice.6
  810.2 24.2 %fusion.150 = f32[128,8192]{1,0:T(8,128)} fusion(s32[1024]{0:T(1024)S(1)} %get-tuple-element.279, s32[128]{0:T(128)S(1)} %get-tuple-element.280, f32[1024,128]{1,0:T(8,128)} %get-tuple-element.276, bf16[12,512,1024]{2,1,0:T(8,128)(2,1)} %get-tuple-element.274, s32[]{:T(128)} %get-tuple-element.251, f32[1024,128]{1,0:T(8,128)} %get-tuple-element.273, ...), kind=kOutput, calls=%fused_computation.30.clone.1 | convolution fusion | flops 2426535936 | bytes 6428160 | tf_op jit(solution)/shard_map/while/body/eval_jaxpr/cr,ck->rk/dot_general | solution.py:85
  834.3 24.0 %fusion.151 = f32[8192]{0:T(1024)S(1)} fusion(f32[128,8192]{1,0:T(8,128)} %fusion.150, s32[128]{0:T(128)S(1)} %get-tuple-element.278, s32[1024]{0:T(1024)S(1)} %get-tuple-element.277, f32[128,1024]{1,0:T(8,128)} %get-tuple-element.272, bf16[12,512,1024]{2,1,0:T(8,128)(2,1)} %get-tuple-element.271, s32[]{:T(128)} %get-tuple-element.251, ...), kind=kOutput, calls=%fused_computation.53.clone.1 | convolution fusion | flops 2428624896 | bytes 6460928 | tf_op jit(solution)/shard_map/while/body/eval_jaxpr/dot_general | solution.py:84
  858.4 1.8 dynamic_update_slice.6
  864.1 0.0 copy-start.4
  864.1 0.0 all-reduce.5.cloned.1.call-update
  864.2 0.1 select_reduce_fusion.1
  864.2 3.1 multiply_reduce_fusion
  867.3 68.3 %all-reduce.5.cloned.1.call-done = f32[12,8192]{1,0:T(8,128)} async-done(((f32[12,8192]{1,0:T(8,128)}), f32[12,8192]{1,0:T(8,128)}) %all-reduce.5.cloned.1.call-update) | async-done | bytes 393232 | tf_op jit(solution)/shard_map/psum | solution.py:119
  935.6 1.2 multiply_reduce_fusion.1
  936.8 0.9 dynamic-slice_multiply_fusion
  937.7 0.0 copy-done.4
  937.7 3.4 fusion.122
  941.1 35.4 %all-reduce = (f32[12,256]{1,0:T(8,128)S(1)}, f32[8,256]{1,0:T(8,128)S(1)}) all-reduce(f32[12,256]{1,0:T(8,128)S(1)} %fusion.122, f32[8,256]{1,0:T(8,128)S(1)} %multiply_reduce_fusion), channel_id=1, replica_groups=mesh['proj'=8,'lang'=4] {'proj'}, use_global_device_ids=true, to_apply=%region_9.10 | all-reduce | flops 5120 | bytes 40960 | tf_op jit(solution)/shard_map/psum | solution.py:132
  976.6 0.1 multiply_reduce_fusion.2
  976.6 0.7 select_reduce_fusion
  (15 shorter events, 0.0 us)
Async XLA Ops:
  8.0 1.0 copy-start
  8.0 10.8 %copy-start.2 = (bf16[1024,128]{1,0:T(8,128)(2,1)S(1)}, bf16[1024,128]{1,0:T(8,128)(2,1)}, u32[]{:S(2)}) copy-start(bf16[1024,128]{1,0:T(8,128)(2,1)} %param.16) | copy-start | bytes 786436
  8.0 231.4 %all-reduce.7.cloned.1.call-start = ((), (), s32[]{:S(2)}) async-start(), calls=%async_computation.2 | async-start | bytes 12582912 | tf_op jit(solution)/shard_map/psum | solution.py:102
  9.0 9.8 copy-start.1
  24.1 1.3 copy-start.5
  24.1 840.1 %all-gather.2.cloned.1.call-start = ((), (), s32[]{:S(2)}) async-start(), calls=%async_computation.1 | async-start | bytes 5242880 | tf_op jit(solution)/shard_map/all_gather | solution.py:127
  24.7 910.9 %all-reduce.5.cloned.1.call-start = ((), (), s32[]{:S(2)}) async-start(), calls=%async_computation | async-start | bytes 1048576 | tf_op jit(solution)/shard_map/psum | solution.py:119
  243.0 621.2 %copy-start.6 = (s32[12,1]{0,1:T(1,128)S(1)}, s32[12,1]{0,1:T(1,128)}, u32[]{:S(2)}) copy-start(s32[12,1]{0,1:T(1,128)} %param.23) | copy-start | bytes 148
  243.0 621.2 %copy-start.7 = (s32[8]{0:T(128)S(1)}, s32[8]{0:T(128)}, u32[]{:S(2)}) copy-start(s32[8]{0:T(128)} %param.24) | copy-start | bytes 100
  864.1 73.6 %copy-start.4 = (f32[12,8]{0,1:T(8,128)S(1)}, f32[12,8]{0,1:T(8,128)}, u32[]{:S(2)}) copy-start(f32[12,8]{0,1:T(8,128)} %convert_convert_fusion) | copy-start | bytes 1156
  937.7 39.6 %copy-start.3 = (f32[12,1024]{1,0:T(8,128)}, f32[12,1024]{1,0:T(8,128)S(1)}, u32[]{:S(2)}) copy-start(f32[12,1024]{1,0:T(8,128)S(1)} %dynamic-slice_multiply_fusion) | copy-start | bytes 147460
Sparse Core Ops, SparseCore 0:
  24.3 215.1 all-reduce.6
  864.3 71.2 all-reduce.4
Sparse Core Ops, SparseCore 1:
  26.2 37.0 all-gather.1
where the time goes:
time: 992 us; the launch traced here: 985 us
  matrix products  597 us (60%)
  waiting for transfers between devices  282 us (28%)
  blocking collectives  35.4 us (4%)
  local copies, waits for them, and re-layouts  22.1 us (2%)
  loops' own time  21.5 us (2%)
  between operations  16.5 us (2%)
  other arithmetic  10.3 us (1%)
    dot_general x12, matrix products, sample_terms(): jnp.einsum('cr,ck->rk', step_down, down_left, preferred_element_type=jnp....  291 us
    dot_general x12, matrix products, sample_terms(): mixed_up = jnp.dot(step_up, up_right, preferred_element_type=jnp.float32)  288 us
    psum x1, waiting for transfers between devices, per_device(): lax.psum((partial_input, partial_gradient), 'proj')  213 us
    psum x1, waiting for transfers between devices, per_device(): summed = lax.psum(projected, 'proj')  68.3 us
    psum x1, blocking collectives, per_device(): dot_sums, val_square = lax.psum((own_part, partial_sq), 'proj')  35.4 us
    another operation x1, loops' own time, per_device(): lax.map(whole_sample, (entering_signal_accumulated, output_slope_accumula...  21.5 us
    dynamic_update_slice x12, local copies, waits for them, and re-layouts, per_device(): lax.map(whole_sample, (entering_signal_accumulated, output_slope_accumula...  21.2 us
  transfers between devices with their start and end apart: 3, of which 2 were waited for; matrix products, arithmetic and copies ran while one was open for 62% of the time, Pallas kernels for 0%

commit v1 on v0

v1 whole, which is shorter than its diff:
```python
import functools
import math

import jax
import jax.numpy as jnp
from jax import lax
from jax.experimental import pallas as pl
from jax.experimental.pallas import tpu as pltpu
from jax.sharding import PartitionSpec as P

RANK = 128
UPDATE_MULTIPLIER = 1.25
M1 = 2146121005
M2_UP = (739982445 * 4 + 2**31) % 2**32 - 2**31


def scramble(hashed):
    hashed = jnp.bitwise_xor(hashed, lax.shift_right_logical(hashed, jnp.int32(16)))
    hashed = hashed * 2146121005
    hashed = jnp.bitwise_xor(hashed, lax.shift_right_logical(hashed, jnp.int32(15)))
    hashed = hashed * 739982445
    hashed = jnp.bitwise_xor(hashed, lax.shift_right_logical(hashed, jnp.int32(16)))
    return hashed


def table_kernel(cols, base_ref, out_ref):
    rows, width = out_ref.shape
    step, piece = 16, 512
    base = base_ref[pl.program_id(0)] + pl.program_id(1) * width
    local = lax.broadcasted_iota(jnp.int32, (step, piece), 0) * cols + lax.broadcasted_iota(
        jnp.int32, (step, piece), 1
    )

    def one(i, carry):
        for j in range(width // piece):
            h = local + (base + i * (step * cols) + j * piece)
            h = h ^ lax.shift_right_logical(h, jnp.int32(16))
            h = h * jnp.int32(M1)
            h = h ^ lax.shift_right_logical(h, jnp.int32(15))
            h = h * jnp.int32(M2_UP)
            h = h ^ lax.shift_left(h, jnp.int32(16))
            sign = jnp.where(h < 0, jnp.float32(-1.0), jnp.float32(1.0))
            out_ref[pl.ds(pl.multiple_of(i * step, step), step), j * piece : (j + 1) * piece] = (
                sign.astype(jnp.bfloat16)
            )
        return carry

    lax.fori_loop(0, rows // step, one, 0)


def sign_tables(bases, cols):
    blocks = bases.shape[0]
    width = 2048
    return pl.pallas_call(
        functools.partial(table_kernel, cols),
        grid=(blocks, cols // width),
        in_specs=[pl.BlockSpec(memory_space=pltpu.SMEM)],
        out_specs=pl.BlockSpec((128, width), lambda i, j: (i, j)),
        out_shape=jax.ShapeDtypeStruct((blocks * 128, cols), jnp.bfloat16),
        cost_estimate=pl.CostEstimate(
            flops=blocks * 128 * cols * 12, bytes_accessed=blocks * 256 * cols, transcendentals=0
        ),
        name="sign_tables",
    )(bases)


def step_kernel(x_ref, g_ref, lx_ref, lg_ref, ml_ref, vl_ref, mr_ref, vr_ref, up_ref, dn_ref):
    def one(low, wide, moment, second, out):
        grad = lax.dot_general(
            low[0], wide[0], (((0,), (0,)), ((), ())), preferred_element_type=jnp.float32
        )
        out[...] = (
            (0.9 * moment[...] + 0.1 * grad)
            * lax.rsqrt(0.999 * second[...] + 0.001 * grad * grad)
        ).astype(jnp.bfloat16)

    one(lx_ref, g_ref, mr_ref, vr_ref, up_ref)
    one(lg_ref, x_ref, ml_ref, vl_ref, dn_ref)


def steps(x, g, lx, lg, ml_t, vl_t, mr, vr):
    n, tok, w = x.shape
    wide = pl.BlockSpec((1, tok, w), lambda i: (i, 0, 0))
    low = pl.BlockSpec((1, tok, RANK), lambda i: (i, 0, 0))
    whole = pl.BlockSpec((RANK, w), lambda i: (0, 0))
    out = pl.BlockSpec((RANK, w), lambda i: (i, 0))
    return pl.pallas_call(
        step_kernel,
        grid=(n,),
        in_specs=[wide, wide, low, low, whole, whole, whole, whole],
        out_specs=[out, out],
        out_shape=[jax.ShapeDtypeStruct((n * RANK, w), jnp.bfloat16)] * 2,
        cost_estimate=pl.CostEstimate(
            flops=n * tok * w * RANK * 4, bytes_accessed=n * tok * w * 4, transcendentals=0
        ),
        compiler_params=pltpu.CompilerParams(vmem_limit_bytes=48 * 1024 * 1024),
        name="adam_steps",
    )(x, g, lx, lg, ml_t, vl_t, mr, vr)


def project_kernel(up_ref, dn_ref, tu_ref, td_ref, ul_ref, dr_ref, out_ref):
    n = up_ref.shape[0] // RANK
    mixed_up = jnp.dot(up_ref[...], tu_ref[...], preferred_element_type=jnp.float32)
    mixed_dn = jnp.dot(dn_ref[...], td_ref[...], preferred_element_type=jnp.float32)
    ul = ul_ref[...].astype(jnp.float32)
    dr = dr_ref[...].astype(jnp.float32)
    for i in range(n):
        part = slice(i * RANK, (i + 1) * RANK)
        out_ref[i : i + 1, :] = jnp.sum(
            mixed_up[part] * ul + mixed_dn[part] * dr, axis=0, keepdims=True
        )


def project(up, dn, tables):
    rows, w = up.shape
    n = rows // RANK
    cols = tables.shape[1]
    tile = 256
    edge = 2 * w // RANK
    whole = pl.BlockSpec((rows, w), lambda k: (0, 0))
    return pl.pallas_call(
        project_kernel,
        grid=(cols // tile,),
        in_specs=[
            whole,
            whole,
            pl.BlockSpec((w, tile), lambda k: (0, k)),
            pl.BlockSpec((w, tile), lambda k: (1, k)),
            pl.BlockSpec((RANK, tile), lambda k: (edge, k)),
            pl.BlockSpec((RANK, tile), lambda k: (edge + 1, k)),
        ],
        out_specs=pl.BlockSpec((n, tile), lambda k: (0, k)),
        out_shape=jax.ShapeDtypeStruct((n, cols), jnp.float32),
        cost_estimate=pl.CostEstimate(
            flops=4 * rows * w * cols, bytes_accessed=4 * w * cols + 4 * rows * w, transcendentals=0
        ),
        compiler_params=pltpu.CompilerParams(vmem_limit_bytes=48 * 1024 * 1024),
        name="project",
    )(up, dn, tables, tables, tables, tables)


def per_device(
    mapped_layer_arguments,
    loss_slope_at_result,
    left_lowrank_weights,
    right_lowrank_weights,
    mean_estimate_left,
    variance_estimate_left,
    mean_estimate_right,
    variance_estimate_right,
    heldout_sketched_slopes,
    tongue_label_per_example,
    heldout_example_tally,
    sketch_random_key,
):
    shard_id = lax.axis_index("proj")
    shards = lax.axis_size("proj")
    n, tok, w = mapped_layer_arguments.shape
    K = w * shards
    nval = heldout_sketched_slopes.shape[1]

    part_in = jnp.einsum(
        "ntw,wr->ntr", mapped_layer_arguments, left_lowrank_weights,
        preferred_element_type=jnp.float32,
    ).astype(jnp.bfloat16)
    part_gr = jnp.einsum(
        "ntw,rw->ntr", loss_slope_at_result, right_lowrank_weights,
        preferred_element_type=jnp.float32,
    ).astype(jnp.bfloat16)
    parts = jnp.stack([part_in, part_gr]).reshape(2, n * tok, RANK)
    share = lax.psum_scatter(parts, "proj", scatter_dimension=1, tiled=True)
    share = (UPDATE_MULTIPLIER * share.astype(jnp.float32)).astype(jnp.bfloat16)
    low = lax.all_gather(share, "proj", axis=1, tiled=True).reshape(2, n, tok, RANK)

    seed4 = sketch_random_key[0] * 4
    inner = jnp.arange(w // RANK, dtype=jnp.int32) * (RANK * K) + shard_id * (w * K)
    bases = jnp.concatenate([
        scramble(seed4 + 1) + inner,
        scramble(seed4 + 2) + inner,
        scramble(seed4)[None],
        scramble(seed4 + 3)[None],
    ])
    tables = sign_tables(bases, K)

    up, dn = steps(
        mapped_layer_arguments, loss_slope_at_result, low[0], low[1],
        mean_estimate_left.T, variance_estimate_left.T, mean_estimate_right, variance_estimate_right,
    )
    projected = project(up, dn, tables)

    all_val = lax.all_gather(heldout_sketched_slopes, "lang", axis=0, tiled=True)
    val_wide = all_val.astype(jnp.float32)
    val_square = lax.psum(jnp.sum(val_wide * val_wide, axis=-1), "proj")

    raw = lax.psum_scatter(projected, "proj", scatter_dimension=1, tiled=True)
    lang_of = tongue_label_per_example[:, 0]
    num_langs = heldout_example_tally.shape[0]
    one_hot = (lang_of[:, None] == lax.iota(jnp.int32, num_langs)[None, :]).astype(jnp.float32)
    partial_all = jnp.einsum(
        "nc,ljc->nlj", raw.astype(jnp.bfloat16), all_val, preferred_element_type=jnp.float32
    )
    own_part = jnp.sum(partial_all * one_hot[:, :, None], axis=1)
    own_square = jnp.sum(raw * raw, axis=-1, keepdims=True)
    sums = lax.psum(jnp.concatenate([own_part, jnp.broadcast_to(own_square, (n, RANK))], axis=1), "proj")
    inverse = lax.rsqrt(sums[:, nval : nval + 1] / K + 1e-06)
    features = raw * inverse
    rms_all = jnp.sqrt(val_square / K + 1e-06)
    rms_own = jnp.sum(one_hot[:, :, None] * rms_all[None, :, :], axis=1)
    count_own = jnp.sum(one_hot.astype(jnp.int32) * heldout_example_tally[None, :], axis=1)
    similar = sums[:, :nval] * inverse / (math.sqrt(K) * rms_own)
    is_valid = lax.iota(jnp.int32, nval)[None, :] < count_own[:, None]
    scores = jnp.max(jnp.where(is_valid, similar, jnp.float32(-1e30)), axis=-1)
    return (features, scores)


def solution(mesh):
    in_specs = (
        P("lang", None, "proj"),
        P("lang", None, "proj"),
        P("proj", None),
        P(None, "proj"),
        P("proj", None),
        P("proj", None),
        P(None, "proj"),
        P(None, "proj"),
        P("lang", None, "proj"),
        P("lang", None),
        P(),
        P(),
    )
    out_specs = (P("lang", "proj"), P("lang"))
    return jax.shard_map(
        per_device, mesh=mesh, in_specs=in_specs, out_specs=out_specs, check_vma=False
    )
```

time: 992 us -> 354 us (0.36)
  matrix products: 597 us -> 15.3 us
  waiting for transfers between devices: 282 us -> 147 us
  Pallas kernels: 0 us -> 125 us
  loops' own time: 21.5 us -> 0 us
  local copies, waits for them, and re-layouts: 22.1 us -> 5.4 us
    dot_general x27 -> x3, matrix products: 597 us -> 15.3 us  [the longest x1 8.16 us: per_device(): jnp.einsum('ntw,rw->ntr', loss_slope_at_result, right_lowrank_weights, pr...]
    psum x2 -> x0, waiting for transfers between devices: 282 us -> none  [the longest x1 213 us: per_device(): lax.psum((partial_input, partial_gradient), 'proj')]
    reduce_scatter x0 -> x2, waiting for transfers between devices: none -> 135 us  [the longest x1 77.2 us: per_device(): share = lax.psum_scatter(parts, 'proj', scatter_dimension=1, tiled=True)]
    pallas_call x0 -> x3, Pallas kernels: none -> 125 us  [the longest x1 62.6 us: project(): pl.pallas_call(project_kernel, grid=(cols // tile,), in_specs=[whole, who...]
    another operation x1 -> x0, loops' own time: 21.5 us -> none  [per_device(): lax.map(whole_sample, (entering_signal_accumulated, output_slope_accumula...]
    dynamic_update_slice x12 -> x0, local copies, waits for them, and re-layouts: 21.2 us -> none  [per_device(): lax.map(whole_sample, (entering_signal_accumulated, output_slope_accumula...]
    all_gather x0 -> x1, waiting for transfers between devices: none -> 11.2 us  [per_device(): lax.all_gather(share, 'proj', axis=1, tiled=True).reshape(2, n, tok, RANK)]
  transfers between devices with their start and end apart: 3 -> 4, of which waited for: 2 -> 3; matrix products, arithmetic and copies ran while one was open for 62% -> 2% of each run, Pallas kernels for 0% -> 36%
where the time goes in v1:
time: 354 us; the launch traced here: 353 us
  waiting for transfers between devices  147 us (42%)
  Pallas kernels  125 us (35%)
  blocking collectives  35.2 us (10%)
  matrix products  15.3 us (4%)
  between operations  14.6 us (4%)
  other arithmetic  10.2 us (3%)
  local copies, waits for them, and re-layouts  5.4 us (2%)
    reduce_scatter x1, waiting for transfers between devices, per_device(): share = lax.psum_scatter(parts, 'proj', scatter_dimension=1, tiled=True)  77.2 us
    pallas_call x1, Pallas kernels, project(): pl.pallas_call(project_kernel, grid=(cols // tile,), in_specs=[whole, who...  62.6 us
    reduce_scatter x1, waiting for transfers between devices, per_device(): raw = lax.psum_scatter(projected, 'proj', scatter_dimension=1, tiled=True)  57.5 us
    pallas_call x1, Pallas kernels, sign_tables(): pl.pallas_call(functools.partial(table_kernel, cols), grid=(blocks, cols...  46.1 us
    psum x1, blocking collectives, per_device(): lax.psum(jnp.concatenate([own_part, jnp.broadcast_to(own_square, (n, RANK...  35.2 us
    pallas_call x1, Pallas kernels, steps(): pl.pallas_call(step_kernel, grid=(n,), in_specs=[wide, wide, low, low, wh...  16.7 us
    all_gather x1, waiting for transfers between devices, per_device(): lax.all_gather(share, 'proj', axis=1, tiled=True).reshape(2, n, tok, RANK)  11.2 us
    dot_general x1, matrix products, per_device(): jnp.einsum('ntw,rw->ntr', loss_slope_at_result, right_lowrank_weights, pr...  8.16 us
  transfers between devices with their start and end apart: 4, of which 3 were waited for; matrix products, arithmetic and copies ran while one was open for 2% of the time, Pallas kernels for 36%

profile of v1, /device:TPU:0, one launch (start us, length us, event | category | flops | bytes accessed | tf_op | source)
XLA Modules:
  0.0 353.1 jit_solution(2450268279307031716)
XLA Ops:
  7.2 0.0 copy-start
  7.2 0.0 copy-start.10
  7.2 0.0 reduce-scatter.3.cloned.1.call-start
  7.2 0.9 copy-done
  8.1 0.0 copy-start.5
  8.1 8.2 %convolution_convert_fusion = bf16[12,512,128]{2,1,0:T(8,128)(2,1)S(1)} fusion(bf16[12,512,1024]{2,1,0:T(8,128)(2,1)} %g_ref.1, bf16[128,1024]{1,0:T(8,128)(2,1)S(1)} %copy-done), kind=kOutput, calls=%fused_computation.2 | convolution fusion | flops 1611399168 | bytes 14417920 | tf_op jit(solution)/shard_map/ntw,rw->ntr/dot_general | solution.py:166
  16.3 0.0 copy-done.10
  16.3 0.0 copy-done.5
  16.3 3.7 %convolution_convert_fusion.1 = bf16[12,512,128]{2,1,0:T(8,128)(2,1)S(1)} fusion(bf16[12,512,1024]{2,1,0:T(8,128)(2,1)S(1)} %copy-done.5, bf16[1024,128]{1,0:T(8,128)(2,1)S(1)} %copy-done.10), kind=kOutput, calls=%fused_computation.3 | convolution fusion | flops 1611399168 | bytes 14417920 | tf_op jit(solution)/shard_map/ntw,wr->ntr/dot_general | solution.py:162
  20.1 1.9 pad_maximum_fusion
  22.0 0.0 copy-start.7
  22.0 0.0 copy-start.8
  22.0 0.0 reduce-scatter.3.cloned.1.call-update
  22.0 0.0 all-gather.3.cloned.1.call-start
  22.1 77.2 %reduce-scatter.3.cloned.1.call-done = bf16[2,768,128]{2,1,0:T(8,128)(2,1)} async-done(((bf16[2,6144,128]{2,1,0:T(8,128)(2,1)}), bf16[2,768,128]{2,1,0:T(8,128)(2,1)}) %reduce-scatter.3.cloned.1.call-update) | async-done | bytes 393232 | tf_op jit(solution)/shard_map/reduce_scatter | solution.py:171
  99.3 1.8 multiply_convert_fusion
  101.1 0.0 all-gather.3.cloned.1.call-update
  101.2 0.0 all-gather.5.cloned.1.call-start
  101.2 0.7 all-gather.5.cloned.1.call-update
  101.9 0.2 reduce-scatter.5.cloned.1.call-start
  102.1 0.0 copy-done.7
  102.1 0.2 copy.18
  102.3 0.0 copy-done.8
  102.4 0.2 copy.19
  103.2 0.6 pad_add_fusion.base_ref
  103.8 46.1 %sign_tables.1.tu_ref.td_ref.ul_ref.dr_ref = bf16[2304,8192]{1,0:T(8,128)(2,1)} custom-call(s32[18]{0:T(128)} %pad_add_fusion.base_ref), custom_call_target="tpu_custom_call" | custom-call | flops 226492416 | bytes 37748736 | tf_op jit(solution)/shard_map/sign_tables/pallas_call | solution.py:54
  149.9 0.0 copy-start.2
  149.9 0.0 copy-start.3
  149.9 11.2 %all-gather.3.cloned.1.call-done = bf16[2,6144,128]{2,1,0:T(8,128)(2,1)} async-done(((bf16[2,768,128]{2,1,0:T(8,128)(2,1)}), bf16[2,6144,128]{2,1,0:T(8,128)(2,1)}) %all-gather.3.cloned.1.call-update) | async-done | bytes 3145744 | tf_op jit(solution)/shard_map/all_gather | solution.py:173
  161.1 2.1 fusion.14
  163.2 0.0 copy-done.2
  163.2 0.0 copy-done.3
  163.2 16.7 %adam_steps.1 = (bf16[1536,1024]{1,0:T(8,128)(2,1)}, bf16[1536,1024]{1,0:T(8,128)(2,1)}) custom-call(bf16[12,512,1024]{2,1,0:T(8,128)(2,1)} %x_ref.1, bf16[12,512,1024]{2,1,0:T(8,128)(2,1)} %g_ref.1, bf16[12,512,128]{2,1,0:T(8,128)(2,1)S(1)} %bitcast.23, bf16[12,512,128]{2,1,0:T(8,128)(2,1)S(1)} %bitcast.22, f32[128,1024]{1,0:T(8,128)S(1)} %bitcast.24, ...), custom_call_target="tpu_custom_call" | custom-call | flops 3221225472 | bytes 25165824 | tf_op jit(solution)/shard_map/adam_steps/pallas_call | solution.py:87
  179.9 0.0 copy-start.4
  179.9 1.9 copy-done.4
  181.8 0.0 copy-start.9
  181.8 0.0 copy-start.11
  181.8 62.6 %project.1 = f32[12,8192]{1,0:T(8,128)} custom-call(bf16[1536,1024]{1,0:T(8,128)(2,1)S(1)} %copy-done.4, bf16[1536,1024]{1,0:T(8,128)(2,1)} %get-tuple-element.5.dn_ref, bf16[2304,8192]{1,0:T(8,128)(2,1)} %sign_tables.1.tu_ref.td_ref.ul_ref.dr_ref, bf16[2304,8192]{1,0:T(8,128)(2,1)} %sign_tables.1.tu_ref.td_ref.ul_ref.dr_ref, ...), custom_call_target="tpu_custom_call" | custom-call | flops 51539607552 | bytes 39845888 | tf_op jit(solution)/shard_map/project/pallas_call | solution.py:121
  244.4 0.0 reduce-scatter.5.cloned.1.call-update
  244.4 0.0 copy-done.9
  244.5 0.0 copy-done.11
  244.5 0.1 multiply_reduce_fusion.3
  244.6 0.0 all-gather.5.cloned.1.call-done
  244.6 0.0 copy-start.1
  244.6 3.1 multiply_reduce_fusion
  247.7 57.5 %reduce-scatter.5.cloned.1.call-done = f32[12,1024]{1,0:T(8,128)} async-done(((f32[12,8192]{1,0:T(8,128)}), f32[12,1024]{1,0:T(8,128)}) %reduce-scatter.5.cloned.1.call-update) | async-done | bytes 49168 | tf_op jit(solution)/shard_map/reduce_scatter | solution.py:195
  305.3 0.0 copy-start.6
  305.3 1.0 multiply_reduce_fusion.2
  306.3 3.4 fusion
  309.7 0.1 broadcast_in_dim.11
  309.8 35.2 %all-reduce = (f32[12,384]{1,0:T(8,128)S(1)}, f32[8,256]{1,0:T(8,128)S(1)}) all-reduce(f32[12,384]{1,0:T(8,128)S(1)} %pad_maximum_fusion.1, f32[8,256]{1,0:T(8,128)S(1)} %multiply_reduce_fusion), channel_id=1, replica_groups=mesh['proj'=8,'lang'=4] {'proj'}, use_global_device_ids=true, to_apply=%region_4.0 | all-reduce | flops 6656 | bytes 53248 | tf_op jit(solution)/shard_map/psum | solution.py:204
  345.0 0.1 fusion.10
  345.1 0.1 multiply_reduce_fusion.1
  345.2 0.7 fusion.7
  345.9 0.0 copy-done.6
  345.9 0.7 broadcast_multiply_fusion
  346.6 0.0 copy-done.1
  (4 shorter events, 0.0 us)
Async XLA Ops:
  7.2 1.0 copy-start
  7.2 9.1 %copy-start.10 = (bf16[1024,128]{1,0:T(8,128)(2,1)S(1)}, bf16[1024,128]{1,0:T(8,128)(2,1)}, u32[]{:S(2)}) copy-start(bf16[1024,128]{1,0:T(8,128)(2,1)} %param.14) | copy-start | bytes 786436
  7.2 92.1 %reduce-scatter.3.cloned.1.call-start = ((), (), s32[]{:S(2)}) async-start(), calls=%async_computation.2 | async-start | bytes 3538944 | tf_op jit(solution)/shard_map/reduce_scatter | solution.py:171
  8.1 8.2 %copy-start.5 = (bf16[12,512,1024]{2,1,0:T(8,128)(2,1)S(1)}, bf16[12,512,1024]{2,1,0:T(8,128)(2,1)}, u32[]{:S(2)}) copy-start(bf16[12,512,1024]{2,1,0:T(8,128)(2,1)} %x_ref.1) | copy-start | bytes 37748740
  22.0 80.1 %copy-start.7 = (f32[1024,128]{1,0:T(8,128)S(1)}, f32[1024,128]{1,0:T(8,128)}, u32[]{:S(2)}) copy-start(f32[1024,128]{1,0:T(8,128)} %param.16) | copy-start | bytes 1572868
  22.0 80.3 %copy-start.8 = (f32[1024,128]{1,0:T(8,128)S(1)}, f32[1024,128]{1,0:T(8,128)}, u32[]{:S(2)}) copy-start(f32[1024,128]{1,0:T(8,128)} %param.17) | copy-start | bytes 1572868
  22.0 139.1 %all-gather.3.cloned.1.call-start = ((), (), s32[]{:S(2)}) async-start(), calls=%async_computation.3 | async-start | bytes 3538944 | tf_op jit(solution)/shard_map/all_gather | solution.py:173
  101.2 143.4 %all-gather.5.cloned.1.call-start = ((), (), s32[]{:S(2)}) async-start(), calls=%async_computation.5 | async-start | bytes 5242880 | tf_op jit(solution)/shard_map/all_gather | solution.py:191
  101.9 203.4 %reduce-scatter.5.cloned.1.call-start = ((), (), s32[]{:S(2)}) async-start(), calls=%async_computation.4 | async-start | bytes 589824 | tf_op jit(solution)/shard_map/reduce_scatter | solution.py:195
  149.9 13.3 %copy-start.2 = (f32[128,1024]{1,0:T(8,128)S(1)}, f32[128,1024]{1,0:T(8,128)}, u32[]{:S(2)}) copy-start(f32[128,1024]{1,0:T(8,128)} %mr_ref.1) | copy-start | bytes 1572868
  149.9 13.3 %copy-start.3 = (f32[128,1024]{1,0:T(8,128)S(1)}, f32[128,1024]{1,0:T(8,128)}, u32[]{:S(2)}) copy-start(f32[128,1024]{1,0:T(8,128)} %vr_ref.1) | copy-start | bytes 1572868
  179.9 1.9 copy-start.4
  181.8 62.7 %copy-start.9 = (s32[12,1]{0,1:T(1,128)S(1)}, s32[12,1]{0,1:T(1,128)}, u32[]{:S(2)}) copy-start(s32[12,1]{0,1:T(1,128)} %param.21) | copy-start | bytes 148
  181.8 62.7 %copy-start.11 = (s32[8]{0:T(128)S(1)}, s32[8]{0:T(128)}, u32[]{:S(2)}) copy-start(s32[8]{0:T(128)} %param.22) | copy-start | bytes 100
  244.6 102.0 %copy-start.1 = (bf16[128,1024]{1,0:T(8,128)(2,1)S(1)}, bf16[128,1024]{1,0:T(8,128)(2,1)}, u32[]{:S(2)}) copy-start(bf16[128,1024]{1,0:T(8,128)(2,1)} %param.15) | copy-start | bytes 786436
  305.3 40.6 %copy-start.6 = (f32[12,1024]{1,0:T(8,128)S(1)}, f32[12,1024]{1,0:T(8,128)}, u32[]{:S(2)}) copy-start(f32[12,1024]{1,0:T(8,128)} %reduce-scatter.5.cloned.1.call-done) | copy-start | bytes 147460
Sparse Core Ops, SparseCore 0:
  22.1 77.1 reduce-scatter.2
  101.5 59.5 all-gather.2
  162.7 33.0 all-gather.4
  244.6 60.6 reduce-scatter.4

commit v2 on v1

v2 whole, which is shorter than its diff:
```python
import functools
import math

import jax
import jax.numpy as jnp
from jax import lax
from jax.experimental import pallas as pl
from jax.experimental.pallas import tpu as pltpu
from jax.sharding import PartitionSpec as P

RANK = 128
UPDATE_MULTIPLIER = 1.25
M1 = 2146121005
M2_UP = (739982445 * 4 + 2**31) % 2**32 - 2**31


def scramble(hashed):
    hashed = jnp.bitwise_xor(hashed, lax.shift_right_logical(hashed, jnp.int32(16)))
    hashed = hashed * 2146121005
    hashed = jnp.bitwise_xor(hashed, lax.shift_right_logical(hashed, jnp.int32(15)))
    hashed = hashed * 739982445
    hashed = jnp.bitwise_xor(hashed, lax.shift_right_logical(hashed, jnp.int32(16)))
    return hashed


def table_kernel(cols, base_ref, out_ref):
    rows, width = out_ref.shape
    step, piece = 16, 512
    base = base_ref[pl.program_id(0)] + pl.program_id(1) * width
    local = lax.broadcasted_iota(jnp.int32, (step, piece), 0) * cols + lax.broadcasted_iota(
        jnp.int32, (step, piece), 1
    )

    def one(i, carry):
        for j in range(width // piece):
            h = local + (base + i * (step * cols) + j * piece)
            h = h ^ lax.shift_right_logical(h, jnp.int32(16))
            h = h * jnp.int32(M1)
            h = h ^ lax.shift_right_logical(h, jnp.int32(15))
            h = h * jnp.int32(M2_UP)
            h = h ^ lax.shift_left(h, jnp.int32(16))
            sign = jnp.where(h < 0, jnp.float32(-1.0), jnp.float32(1.0))
            out_ref[pl.ds(pl.multiple_of(i * step, step), step), j * piece : (j + 1) * piece] = (
                sign.astype(jnp.bfloat16)
            )
        return carry

    lax.fori_loop(0, rows // step, one, 0)


def sign_tables(bases, cols):
    blocks = bases.shape[0]
    width = 2048
    return pl.pallas_call(
        functools.partial(table_kernel, cols),
        grid=(blocks, cols // width),
        in_specs=[pl.BlockSpec(memory_space=pltpu.SMEM)],
        out_specs=pl.BlockSpec((128, width), lambda i, j: (i, j)),
        out_shape=jax.ShapeDtypeStruct((blocks * 128, cols), jnp.bfloat16),
        cost_estimate=pl.CostEstimate(
            flops=blocks * 128 * cols * 12, bytes_accessed=blocks * 256 * cols, transcendentals=0
        ),
        name="sign_tables",
    )(bases)


def share_kernel(pieces_ref, order_ref, out_ref):
    total = pieces_ref[0].astype(jnp.float32)
    for i in range(1, pieces_ref.shape[0]):
        total = total + pieces_ref[i].astype(jnp.float32)
    out_ref[...] = (UPDATE_MULTIPLIER * total).astype(jnp.bfloat16)


def share_of(pieces, after, name):
    _, rows, rank = pieces.shape
    vmem = pl.BlockSpec(memory_space=pltpu.VMEM)
    return pl.pallas_call(
        share_kernel,
        in_specs=[vmem, pl.BlockSpec(memory_space=pl.ANY)],
        out_specs=vmem,
        out_shape=jax.ShapeDtypeStruct((rows, rank), jnp.bfloat16),
        compiler_params=pltpu.CompilerParams(vmem_limit_bytes=16 * 1024 * 1024),
        name=name,
    )(pieces, after)


def step_kernel(wide_ref, low_ref, moment_ref, second_ref, order_ref, out_ref):
    grad = lax.dot_general(
        low_ref[0], wide_ref[0], (((0,), (0,)), ((), ())), preferred_element_type=jnp.float32
    )
    out_ref[...] = (
        (0.9 * moment_ref[...] + 0.1 * grad)
        * lax.rsqrt(0.999 * second_ref[...] + 0.001 * grad * grad)
    ).astype(jnp.bfloat16)


def steps(wide, low, moment, second, after, name):
    n, tok, w = wide.shape
    whole = pl.BlockSpec((RANK, w), lambda i: (0, 0))
    return pl.pallas_call(
        step_kernel,
        grid=(n,),
        in_specs=[
            pl.BlockSpec((1, tok, w), lambda i: (i, 0, 0)),
            pl.BlockSpec((1, tok, RANK), lambda i: (i, 0, 0)),
            whole,
            whole,
            pl.BlockSpec(memory_space=pl.ANY),
        ],
        out_specs=pl.BlockSpec((RANK, w), lambda i: (i, 0)),
        out_shape=jax.ShapeDtypeStruct((n * RANK, w), jnp.bfloat16),
        cost_estimate=pl.CostEstimate(
            flops=n * tok * w * RANK * 2, bytes_accessed=n * tok * w * 2, transcendentals=0
        ),
        compiler_params=pltpu.CompilerParams(vmem_limit_bytes=32 * 1024 * 1024),
        name=name,
    )(wide, low, moment, second, after)


def project_kernel(has_prior, *refs):
    if has_prior:
        step_ref, table_ref, side_ref, prior_ref, out_ref = refs
    else:
        step_ref, table_ref, side_ref, out_ref = refs
    n = step_ref.shape[0] // RANK
    mixed = jnp.dot(step_ref[...], table_ref[...], preferred_element_type=jnp.float32)
    side = side_ref[...].astype(jnp.float32)
    for i in range(n):
        row = jnp.sum(mixed[i * RANK : (i + 1) * RANK] * side, axis=0, keepdims=True)
        if has_prior:
            row = row + prior_ref[i : i + 1, :]
        out_ref[i : i + 1, :] = row


def project(step, tables, name, prior):
    rows, w = step.shape
    n = rows // RANK
    cols = tables.shape[1]
    tile = min(512, w)
    inner = w // tile
    edge = w // RANK
    out = pl.BlockSpec((None, n, tile), lambda k: (k // inner, 0, k % inner))
    in_specs = [
        pl.BlockSpec((rows, w), lambda k: (0, 0)),
        pl.BlockSpec((w, tile), lambda k: (0, k)),
        pl.BlockSpec((RANK, tile), lambda k: (edge, k)),
    ]
    operands = [step, tables, tables]
    if prior is not None:
        in_specs.append(out)
        operands.append(prior)
    return pl.pallas_call(
        functools.partial(project_kernel, prior is not None),
        grid=(cols // tile,),
        in_specs=in_specs,
        out_specs=out,
        out_shape=jax.ShapeDtypeStruct((cols // w, n, w), jnp.float32),
        cost_estimate=pl.CostEstimate(
            flops=2 * rows * w * cols, bytes_accessed=2 * w * cols + 2 * rows * w, transcendentals=0
        ),
        compiler_params=pltpu.CompilerParams(vmem_limit_bytes=40 * 1024 * 1024),
        name=name,
    )(*operands)


def finish_kernel(
    shards, langs, nval,
    proj_ref, val_ref, hot_ref, square_ref, count_ref,
    feat_ref, score_ref,
    land, message, notes, send1, recv1, send2, recv2,
):
    me = lax.axis_index("proj")
    n, w = feat_ref.shape
    cols = shards * w
    barrier = pltpu.get_barrier_semaphore()
    for d in range(1, shards):
        pl.semaphore_signal(
            barrier, inc=1, device_id={"proj": lax.rem(me + d, shards)},
            device_id_type=pl.DeviceIdType.MESH,
        )
    pl.semaphore_wait(barrier, shards - 1)

    first = []
    for d in range(1, shards):
        target = lax.rem(me + d, shards)
        copy = pltpu.make_async_remote_copy(
            src_ref=proj_ref.at[target], dst_ref=land.at[d - 1],
            send_sem=send1.at[d - 1], recv_sem=recv1.at[d - 1],
            device_id={"proj": target}, device_id_type=pl.DeviceIdType.MESH,
        )
        copy.start()
        first.append(copy)
    message[n:, :] = jnp.zeros((message.shape[0] - n, message.shape[1]), jnp.float32)
    message[16 : 16 + n, :nval] = square_ref[...]
    raw = proj_ref[me]
    for copy in first:
        copy.wait_recv()
    for d in range(1, shards):
        raw = raw + land[d - 1]
    dots = lax.dot_general(
        raw.astype(jnp.bfloat16), val_ref[...], (((1,), (1,)), ((), ())),
        preferred_element_type=jnp.float32,
    )
    own = jnp.zeros((n, nval), jnp.float32)
    for l in range(langs):
        own = own + hot_ref[:, l : l + 1] * dots[:, l * nval : (l + 1) * nval]
    message[:n, :nval] = own
    message[:n, nval:] = jnp.broadcast_to(
        jnp.sum(raw * raw, axis=1, keepdims=True), (n, message.shape[1] - nval)
    )
    second = []
    for d in range(1, shards):
        target = lax.rem(me + d, shards)
        copy = pltpu.make_async_remote_copy(
            src_ref=message, dst_ref=notes.at[d - 1],
            send_sem=send2.at[d - 1], recv_sem=recv2.at[d - 1],
            device_id={"proj": target}, device_id_type=pl.DeviceIdType.MESH,
        )
        copy.start()
        second.append(copy)
    total = message[...]
    for copy in second:
        copy.wait_recv()
    for d in range(1, shards):
        total = total + notes[d - 1]
    inverse = lax.rsqrt(total[:n, nval : nval + 1] / cols + 1e-06)
    feat_ref[...] = raw * inverse
    rms = jnp.sqrt(total[16 : 16 + n, :nval] / cols + 1e-06)
    similar = total[:n, :nval] * inverse / (math.sqrt(cols) * rms)
    live = lax.broadcasted_iota(jnp.int32, (n, nval), 1) < count_ref[...]
    best = jnp.max(jnp.where(live, similar, jnp.float32(-1e30)), axis=1, keepdims=True)
    score_ref[...] = jnp.broadcast_to(best, score_ref.shape)
    for copy in first + second:
        copy.wait_send()


def finish(projected, all_val, hot, own_square, count):
    shards, n, w = projected.shape
    langs, nval = all_val.shape[0], all_val.shape[1]
    vmem = pl.BlockSpec(memory_space=pltpu.VMEM)
    return pl.pallas_call(
        functools.partial(finish_kernel, shards, langs, nval),
        in_specs=[vmem] * 5,
        out_specs=[vmem] * 2,
        out_shape=[
            jax.ShapeDtypeStruct((n, w), jnp.float32),
            jax.ShapeDtypeStruct((n, 128), jnp.float32),
        ],
        scratch_shapes=[
            pltpu.VMEM((shards - 1, n, w), jnp.float32),
            pltpu.VMEM((32, nval + 128), jnp.float32),
            pltpu.VMEM((shards - 1, 32, nval + 128), jnp.float32),
            pltpu.SemaphoreType.DMA((shards - 1,)),
            pltpu.SemaphoreType.DMA((shards - 1,)),
            pltpu.SemaphoreType.DMA((shards - 1,)),
            pltpu.SemaphoreType.DMA((shards - 1,)),
        ],
        compiler_params=pltpu.CompilerParams(
            collective_id=0, has_side_effects=True, vmem_limit_bytes=32 * 1024 * 1024
        ),
        name="finish",
    )(projected, all_val.reshape(langs * nval, w), hot, own_square, count)


def per_device(
    mapped_layer_arguments,
    loss_slope_at_result,
    left_lowrank_weights,
    right_lowrank_weights,
    mean_estimate_left,
    variance_estimate_left,
    mean_estimate_right,
    variance_estimate_right,
    heldout_sketched_slopes,
    tongue_label_per_example,
    heldout_example_tally,
    sketch_random_key,
):
    shard_id = lax.axis_index("proj")
    shards = lax.axis_size("proj")
    n, tok, w = mapped_layer_arguments.shape
    K = w * shards

    part_in = jnp.einsum(
        "ntw,wr->ntr", mapped_layer_arguments, left_lowrank_weights,
        preferred_element_type=jnp.float32,
    ).astype(jnp.bfloat16)
    part_gr = jnp.einsum(
        "ntw,rw->ntr", loss_slope_at_result, right_lowrank_weights,
        preferred_element_type=jnp.float32,
    ).astype(jnp.bfloat16)

    def pieces_of(part):
        return lax.all_to_all(
            part.reshape(shards, n * tok // shards, RANK), "proj", split_axis=0, concat_axis=0
        )

    def gather(share):
        return lax.all_gather(share, "proj", axis=0, tiled=True).reshape(n, tok, RANK)

    seed4 = sketch_random_key[0] * 4
    inner = jnp.arange(w // RANK, dtype=jnp.int32) * (RANK * K) + shard_id * (w * K)
    tables = [
        sign_tables(
            jnp.concatenate([scramble(seed4 + wide) + inner, scramble(seed4 + narrow)[None]]), K
        )
        for wide, narrow in ((1, 0), (2, 3))
    ]
    low_in = gather(share_of(pieces_of(part_in), tables[0], "share_in"))
    low_gr = gather(share_of(pieces_of(part_gr), tables[1], "share_gr"))

    up = steps(
        loss_slope_at_result, low_in, mean_estimate_right, variance_estimate_right, tables[1],
        "steps_up"
    )
    half = project(up, tables[0], "project_up", None)
    dn = steps(
        mapped_layer_arguments, low_gr, mean_estimate_left.T, variance_estimate_left.T, half,
        "steps_down"
    )
    projected = project(dn, tables[1], "project_down", half)

    all_val = lax.all_gather(heldout_sketched_slopes, "lang", axis=0, tiled=True)
    val_wide = all_val.astype(jnp.float32)
    val_square = jnp.sum(val_wide * val_wide, axis=-1)
    lang_of = tongue_label_per_example[:, 0]
    num_langs = heldout_example_tally.shape[0]
    hot = (lang_of[:, None] == lax.iota(jnp.int32, num_langs)[None, :]).astype(jnp.float32)
    own_square = jnp.sum(hot[:, :, None] * val_square[None, :, :], axis=1)
    count_own = jnp.sum(
        hot.astype(jnp.int32) * heldout_example_tally[None, :], axis=1, keepdims=True
    )
    features, scores = finish(projected, all_val, hot, own_square, count_own)
    scores = scores[:, 0]
    return (features, scores)


def solution(mesh):
    in_specs = (
        P("lang", None, "proj"),
        P("lang", None, "proj"),
        P("proj", None),
        P(None, "proj"),
        P("proj", None),
        P("proj", None),
        P(None, "proj"),
        P(None, "proj"),
        P("lang", None, "proj"),
        P("lang", None),
        P(),
        P(),
    )
    out_specs = (P("lang", "proj"), P("lang"))
    return jax.shard_map(
        per_device, mesh=mesh, in_specs=in_specs, out_specs=out_specs, check_vma=False
    )
```

time: 354 us -> 252 us (0.71)
  waiting for transfers between devices: 147 us -> 26.3 us
  blocking collectives: 35.2 us -> 0 us
  local copies, waits for them, and re-layouts: 5.4 us -> 30.9 us
  Pallas kernels: 125 us -> 145 us
  starting transfers between devices: 0.34 us -> 11.2 us
  other arithmetic: 10.2 us -> 4.79 us
    reduce_scatter x2 -> x0, waiting for transfers between devices: 135 us -> none  [the longest x1 77.2 us: per_device(): share = lax.psum_scatter(parts, 'proj', scatter_dimension=1, tiled=True)]
    psum x1 -> x0, blocking collectives: 35.2 us -> none  [per_device(): lax.psum(jnp.concatenate([own_part, jnp.broadcast_to(own_square, (n, RANK...]
    unnamed x26 -> x31, local copies, waits for them, and re-layouts: 3.23 us -> 30.1 us
    pallas_call x2 -> x7, Pallas kernels: 79.3 us -> 97.6 us  [the longest x2 62 us: project(): pl.pallas_call(functools.partial(project_kernel, prior is not None), grid...]
    all_to_all x0 -> x2, waiting for transfers between devices: none -> 14.7 us  [pieces_of(): lax.all_to_all(part.reshape(shards, n * tok // shards, RANK), 'proj', spl...]
    all_to_all x0 -> x2, starting transfers between devices: none -> 10.9 us  [pieces_of(): lax.all_to_all(part.reshape(shards, n * tok // shards, RANK), 'proj', spl...]
    dot_general x1, matrix products: 3.74 us -> 9.17 us  [per_device(): jnp.einsum('ntw,wr->ntr', mapped_layer_arguments, left_lowrank_weights, p...]
    pallas_call x1 -> x2, Pallas kernels: 46.1 us -> 47.4 us  [sign_tables(): pl.pallas_call(functools.partial(table_kernel, cols), grid=(blocks, cols...]
  transfers between devices with their start and end apart: 4 -> 5, of which waited for: 3 -> 4; matrix products, arithmetic and copies ran while one was open for 2% -> 5% of each run, Pallas kernels for 36% -> 48%
where the time goes in v2:
time: 252 us; the launch traced here: 251 us
  Pallas kernels  145 us (58%)
  local copies, waits for them, and re-layouts  30.9 us (12%)
  waiting for transfers between devices  26.3 us (10%)
  matrix products  18.3 us (7%)
  between operations  14.6 us (6%)
  starting transfers between devices  11.2 us (4%)
  other arithmetic  4.79 us (2%)
    pallas_call x2, Pallas kernels, project(): pl.pallas_call(functools.partial(project_kernel, prior is not None), grid...  62 us
    pallas_call x2, Pallas kernels, sign_tables(): pl.pallas_call(functools.partial(table_kernel, cols), grid=(blocks, cols...  47.4 us
    unnamed x31, local copies, waits for them, and re-layouts  30.1 us
    pallas_call x1, Pallas kernels, finish(): pl.pallas_call(functools.partial(finish_kernel, shards, langs, nval), in_...  24.2 us
    all_to_all x2, waiting for transfers between devices, pieces_of(): lax.all_to_all(part.reshape(shards, n * tok // shards, RANK), 'proj', spl...  14.7 us
    all_gather x2, waiting for transfers between devices, gather(): lax.all_gather(share, 'proj', axis=0, tiled=True).reshape(n, tok, RANK)  11 us
    all_to_all x2, starting transfers between devices, pieces_of(): lax.all_to_all(part.reshape(shards, n * tok // shards, RANK), 'proj', spl...  10.9 us
    pallas_call x2, Pallas kernels, steps(): pl.pallas_call(step_kernel, grid=(n,), in_specs=[pl.BlockSpec((1, tok, w)...  9.67 us
  transfers between devices with their start and end apart: 5, of which 4 were waited for; matrix products, arithmetic and copies ran while one was open for 5% of the time, Pallas kernels for 48%

profile of v2, /device:TPU:0, one launch (start us, length us, event | category | flops | bytes accessed | tf_op | source)
XLA Modules:
  0.0 251.0 jit_solution(8956172358404351705)
XLA Ops:
  7.2 0.0 copy-start
  7.2 0.9 copy-done
  8.1 9.2 %convolution_convert_fusion = bf16[12,512,128]{2,1,0:T(8,128)(2,1)} fusion(bf16[12,512,1024]{2,1,0:T(8,128)(2,1)} %wide_ref.3, bf16[1024,128]{1,0:T(8,128)(2,1)S(1)} %copy-done), kind=kOutput, calls=%fused_computation.1 | convolution fusion | flops 1611399168 | bytes 14417920 | tf_op jit(solution)/shard_map/ntw,wr->ntr/dot_general | solution.py:284
  17.3 7.3 %all-to-all-start.1 = ((bf16[8,768,128]{2,1,0:T(8,128)(2,1)}), bf16[8,768,128]{2,1,0:T(8,128)(2,1)S(1)}, u32[]{:S(2)}, u32[]{:S(2)}) async-start(bf16[8,768,128]{2,1,0:T(8,128)(2,1)} %bitcast.8), calls=%async_computation.1 | async-start | bytes 3145728 | tf_op jit(solution)/shard_map/all_to_all | solution.py:294
  25.2 0.6 pad_add_fusion.1.base_ref
  25.8 0.0 copy-start.12
  25.9 23.8 %sign_tables.3.order_ref.refs_1_.refs_2_ = bf16[1152,8192]{1,0:T(8,128)(2,1)} custom-call(s32[9]{0:T(128)} %pad_add_fusion.1.base_ref), custom_call_target="tpu_custom_call" | custom-call | flops 113246208 | bytes 18874368 | tf_op jit(solution)/shard_map/sign_tables/pallas_call | solution.py:54
  49.6 0.0 copy-done.12
  49.6 9.1 %convolution_convert_fusion.1 = bf16[12,512,128]{2,1,0:T(8,128)(2,1)} fusion(bf16[12,512,1024]{2,1,0:T(8,128)(2,1)} %wide_ref.2, bf16[128,1024]{1,0:T(8,128)(2,1)S(1)} %copy-done.12), kind=kOutput, calls=%fused_computation.2 | convolution fusion | flops 1611399168 | bytes 14417920 | tf_op jit(solution)/shard_map/ntw,rw->ntr/dot_general | solution.py:288
  58.8 2.8 %all-to-all-done.1.pieces_ref = bf16[8,768,128]{2,1,0:T(8,128)(2,1)S(1)} async-done(((bf16[8,768,128]{2,1,0:T(8,128)(2,1)}), bf16[8,768,128]{2,1,0:T(8,128)(2,1)S(1)}, u32[]{:S(2)}, u32[]{:S(2)}) %all-to-all-start.1) | async-done | bytes 1572896 | tf_op jit(solution)/shard_map/all_to_all | solution.py:294
  61.6 3.6 %all-to-all-start = ((bf16[8,768,128]{2,1,0:T(8,128)(2,1)}), bf16[8,768,128]{2,1,0:T(8,128)(2,1)S(1)}, u32[]{:S(2)}, u32[]{:S(2)}) async-start(bf16[8,768,128]{2,1,0:T(8,128)(2,1)} %bitcast.25), calls=%async_computation | async-start | bytes 3145728 | tf_op jit(solution)/shard_map/all_to_all | solution.py:294
  65.2 0.0 all-gather.6.cloned.1.call-start
  65.2 0.0 copy-start.3
  65.2 6.4 %copy-done.3 = bf16[1152,8192]{1,0:T(8,128)(2,1)S(1)} copy-done((bf16[1152,8192]{1,0:T(8,128)(2,1)S(1)}, bf16[1152,8192]{1,0:T(8,128)(2,1)}, u32[]{:S(2)}) %copy-start.3) | copy-done | bytes 18874392
  71.6 0.9 share_in.1
  72.5 0.0 all-gather.6.cloned.1.call-update
  72.5 0.0 all-gather.4.cloned.1.call-start
  72.6 0.6 pad_add_fusion.base_ref
  73.2 23.6 %sign_tables.2.order_ref.refs_1_.refs_2_ = bf16[1152,8192]{1,0:T(8,128)(2,1)} custom-call(s32[9]{0:T(128)} %pad_add_fusion.base_ref), custom_call_target="tpu_custom_call" | custom-call | flops 113246208 | bytes 18874368 | tf_op jit(solution)/shard_map/sign_tables/pallas_call | solution.py:54
  96.8 11.9 %all-to-all-done.pieces_ref = bf16[8,768,128]{2,1,0:T(8,128)(2,1)S(1)} async-done(((bf16[8,768,128]{2,1,0:T(8,128)(2,1)}), bf16[8,768,128]{2,1,0:T(8,128)(2,1)S(1)}, u32[]{:S(2)}, u32[]{:S(2)}) %all-to-all-start) | async-done | bytes 1572896 | tf_op jit(solution)/shard_map/all_to_all | solution.py:294
  108.7 0.0 copy-start.2
  108.7 6.6 %copy-done.2 = bf16[1152,8192]{1,0:T(8,128)(2,1)S(1)} copy-done((bf16[1152,8192]{1,0:T(8,128)(2,1)S(1)}, bf16[1152,8192]{1,0:T(8,128)(2,1)}, u32[]{:S(2)}) %copy-start.2) | copy-done | bytes 18874392
  115.3 0.0 copy-start.11
  115.3 0.0 copy-start.13
  115.3 0.0 copy-start.9
  115.3 0.9 share_gr.1
  116.2 0.0 all-gather.4.cloned.1.call-update
  116.2 0.2 all-gather.8.cloned.1.call-start
  116.4 0.5 all-gather.8.cloned.1.call-update
  116.9 1.2 copy.23
  118.2 1.2 copy.24
  119.4 0.0 copy-done.11
  119.4 0.0 copy-done.13
  119.4 0.2 multiply_reduce_fusion.2
  119.6 0.1 copy.25.count_ref
  119.7 0.1 fusion.2.hot_ref
  119.8 8.9 %all-gather.6.cloned.1.call-done = bf16[6144,128]{1,0:T(8,128)(2,1)} async-done(((bf16[768,128]{1,0:T(8,128)(2,1)}), bf16[6144,128]{1,0:T(8,128)(2,1)}) %all-gather.6.cloned.1.call-update) | async-done | bytes 1572880 | tf_op jit(solution)/shard_map/all_gather | solution.py:299
  128.7 0.0 copy-done.9
  128.7 0.0 copy-start.6
  128.7 4.6 %copy-done.6 = bf16[12,512,1024]{2,1,0:T(8,128)(2,1)S(1)} copy-done((bf16[12,512,1024]{2,1,0:T(8,128)(2,1)S(1)}, bf16[12,512,1024]{2,1,0:T(8,128)(2,1)}, u32[]{:S(2)}) %copy-start.6) | copy-done | bytes 12582936
  133.3 0.0 copy-start.7
  133.3 1.4 copy-done.7
  134.7 0.0 copy-start.10
  134.7 1.0 copy-done.10
  135.7 4.8 %steps_up.1.refs_0_ = bf16[1536,1024]{1,0:T(8,128)(2,1)S(1)} custom-call(bf16[12,512,1024]{2,1,0:T(8,128)(2,1)S(1)} %copy-done.6, bf16[12,512,128]{2,1,0:T(8,128)(2,1)S(1)} %bitcast.23, f32[128,1024]{1,0:T(8,128)S(1)} %copy-done.9, f32[128,1024]{1,0:T(8,128)S(1)} %copy-done.10, bf16[1152,8192]{1,0:T(8,128)(2,1)} %sign_tables.2.order_ref.refs_1_.refs_2_), custom_call_target="tpu_custom_call" | custom-call | flops 1610612736 | bytes 12582912 | tf_op jit(solution)/shard_map/steps_up/pallas_call | solution.py:100
  140.5 30.9 %project_up.1.order_ref.refs_3_ = f32[8,12,1024]{2,1,0:T(8,128)S(1)} custom-call(bf16[1536,1024]{1,0:T(8,128)(2,1)S(1)} %steps_up.1.refs_0_, bf16[1152,8192]{1,0:T(8,128)(2,1)} %sign_tables.3.order_ref.refs_1_.refs_2_, bf16[1152,8192]{1,0:T(8,128)(2,1)} %sign_tables.3.order_ref.refs_1_.refs_2_), custom_call_target="tpu_custom_call" | custom-call | flops 25769803776 | bytes 19922944 | tf_op jit(solution)/shard_map/project_up/pallas_call | solution.py:152
  171.5 2.1 all-gather.4.cloned.1.call-done
  173.6 0.0 copy-start.5
  173.6 4.6 %copy-done.5 = bf16[12,512,1024]{2,1,0:T(8,128)(2,1)S(1)} copy-done((bf16[12,512,1024]{2,1,0:T(8,128)(2,1)S(1)}, bf16[12,512,1024]{2,1,0:T(8,128)(2,1)}, u32[]{:S(2)}) %copy-start.5) | copy-done | bytes 12582936
  178.1 0.0 copy-start.8
  178.2 1.4 copy-done.8
  179.6 4.9 %steps_down.1.refs_0_ = bf16[1536,1024]{1,0:T(8,128)(2,1)S(1)} custom-call(bf16[12,512,1024]{2,1,0:T(8,128)(2,1)S(1)} %copy-done.5, bf16[12,512,128]{2,1,0:T(8,128)(2,1)S(1)} %bitcast.24, f32[128,1024]{1,0:T(8,128)S(1)} %bitcast.21, f32[128,1024]{1,0:T(8,128)S(1)} %bitcast.22, f32[8,12,1024]{2,1,0:T(8,128)S(1)} %project_up.1.order_ref.refs_3_), custom_call_target="tpu_custom_call" | custom-call | flops 1610612736 | bytes 12582912 | tf_op jit(solution)/shard_map/steps_down/pallas_call | solution.py:100
  184.4 0.0 copy-start.1
  184.4 31.1 %project_down.1.proj_ref = f32[8,12,1024]{2,1,0:T(8,128)S(1)} custom-call(bf16[1536,1024]{1,0:T(8,128)(2,1)S(1)} %steps_down.1.refs_0_, bf16[1152,8192]{1,0:T(8,128)(2,1)} %sign_tables.2.order_ref.refs_1_.refs_2_, bf16[1152,8192]{1,0:T(8,128)(2,1)} %sign_tables.2.order_ref.refs_1_.refs_2_, f32[8,12,1024]{2,1,0:T(8,128)S(1)} %project_up.1.order_ref.refs_3_), custom_call_target="tpu_custom_call" | custom-call | flops 25769803776 | bytes 19922944 | tf_op jit(solution)/shard_map/project_down/pallas_call | solution.py:152
  215.5 0.0 all-gather.8.cloned.1.call-done
  215.5 0.0 copy-start.4
  215.5 3.2 %multiply_reduce_fusion = f32[8,256]{1,0:T(8,128)S(1)} fusion(bf16[8,256,1024]{2,1,0:T(8,128)(2,1)} %all-gather.8.cloned.1.call-done), kind=kLoop, calls=%fused_computation | loop fusion | flops 6289408 | bytes 4202496 | tf_op jit(solution)/shard_map/reduce_sum | solution.py:325
  218.8 0.1 multiply_reduce_fusion.1.square_ref
  218.9 0.1 copy-done.4
  219.0 24.2 %finish.1 = (f32[12,1024]{1,0:T(8,128)S(1)}, f32[12,128]{1,0:T(8,128)S(1)}) custom-call(f32[8,12,1024]{2,1,0:T(8,128)S(1)} %project_down.1.proj_ref, bf16[2048,1024]{1,0:T(8,128)(2,1)S(1)} %bitcast.20, f32[12,8]{1,0:T(8,128)S(1)} %fusion.2.hot_ref, f32[12,256]{1,0:T(8,128)S(1)} %multiply_reduce_fusion.1.square_ref, s32[12,1]{1,0:T(8,128)S(1)} %copy.25.count_ref), custom_call_target="tpu_custom_call" | custom-call | tf_op jit(solution)/shard_map/finish/pallas_call | solution.py:241
  243.2 0.6 slice_reduce_fusion
  243.9 0.6 copy.28
  244.5 0.0 copy-done.1
  (1 shorter events, 0.0 us)
Async XLA Ops:
  7.2 1.0 copy-start
  17.3 44.3 %all-to-all-start.1 = ((bf16[8,768,128]{2,1,0:T(8,128)(2,1)}), bf16[8,768,128]{2,1,0:T(8,128)(2,1)S(1)}, u32[]{:S(2)}, u32[]{:S(2)}) async-start(bf16[8,768,128]{2,1,0:T(8,128)(2,1)} %bitcast.8), calls=%async_computation.1 | async-start | bytes 3145728 | tf_op jit(solution)/shard_map/all_to_all | solution.py:294
  25.8 23.8 %copy-start.12 = (bf16[128,1024]{1,0:T(8,128)(2,1)S(1)}, bf16[128,1024]{1,0:T(8,128)(2,1)}, u32[]{:S(2)}) copy-start(bf16[128,1024]{1,0:T(8,128)(2,1)} %param.15) | copy-start | bytes 786436
  61.6 47.1 %all-to-all-start = ((bf16[8,768,128]{2,1,0:T(8,128)(2,1)}), bf16[8,768,128]{2,1,0:T(8,128)(2,1)S(1)}, u32[]{:S(2)}, u32[]{:S(2)}) async-start(bf16[8,768,128]{2,1,0:T(8,128)(2,1)} %bitcast.25), calls=%async_computation | async-start | bytes 3145728 | tf_op jit(solution)/shard_map/all_to_all | solution.py:294
  65.2 63.5 %all-gather.6.cloned.1.call-start = ((), (), s32[]{:S(2)}) async-start(), calls=%async_computation.3 | async-start | bytes 1769472 | tf_op jit(solution)/shard_map/all_gather | solution.py:299
  65.2 6.4 %copy-start.3 = (bf16[1152,8192]{1,0:T(8,128)(2,1)S(1)}, bf16[1152,8192]{1,0:T(8,128)(2,1)}, u32[]{:S(2)}) copy-start(bf16[1152,8192]{1,0:T(8,128)(2,1)} %sign_tables.3.order_ref.refs_1_.refs_2_) | copy-start | bytes 56623108
  72.5 101.1 %all-gather.4.cloned.1.call-start = ((), (), s32[]{:S(2)}) async-start(), calls=%async_computation.2 | async-start | bytes 1769472 | tf_op jit(solution)/shard_map/all_gather | solution.py:299
  108.7 6.6 %copy-start.2 = (bf16[1152,8192]{1,0:T(8,128)(2,1)S(1)}, bf16[1152,8192]{1,0:T(8,128)(2,1)}, u32[]{:S(2)}) copy-start(bf16[1152,8192]{1,0:T(8,128)(2,1)} %sign_tables.2.order_ref.refs_1_.refs_2_) | copy-start | bytes 56623108
  115.3 4.2 %copy-start.11 = (s32[12,1]{0,1:T(1,128)S(1)}, s32[12,1]{0,1:T(1,128)}, u32[]{:S(2)}) copy-start(s32[12,1]{0,1:T(1,128)} %param.21) | copy-start | bytes 148
  115.3 4.2 %copy-start.13 = (s32[8]{0:T(128)S(1)}, s32[8]{0:T(128)}, u32[]{:S(2)}) copy-start(s32[8]{0:T(128)} %param.22) | copy-start | bytes 100
  115.3 13.4 %copy-start.9 = (f32[128,1024]{1,0:T(8,128)S(1)}, f32[128,1024]{1,0:T(8,128)}, u32[]{:S(2)}) copy-start(f32[128,1024]{1,0:T(8,128)} %moment_ref.1) | copy-start | bytes 1572868
  116.2 99.3 %all-gather.8.cloned.1.call-start = ((), (), s32[]{:S(2)}) async-start(), calls=%async_computation.4 | async-start | bytes 5242880 | tf_op jit(solution)/shard_map/all_gather | solution.py:323
  128.7 4.6 %copy-start.6 = (bf16[12,512,1024]{2,1,0:T(8,128)(2,1)S(1)}, bf16[12,512,1024]{2,1,0:T(8,128)(2,1)}, u32[]{:S(2)}) copy-start(bf16[12,512,1024]{2,1,0:T(8,128)(2,1)} %wide_ref.2) | copy-start | bytes 37748740
  133.3 1.4 copy-start.7
  134.7 1.0 copy-start.10
  173.6 4.6 %copy-start.5 = (bf16[12,512,1024]{2,1,0:T(8,128)(2,1)S(1)}, bf16[12,512,1024]{2,1,0:T(8,128)(2,1)}, u32[]{:S(2)}) copy-start(bf16[12,512,1024]{2,1,0:T(8,128)(2,1)} %wide_ref.3) | copy-start | bytes 37748740
  178.1 1.4 copy-start.8
  184.4 60.1 %copy-start.1 = (bf16[1024,128]{1,0:T(8,128)(2,1)S(1)}, bf16[1024,128]{1,0:T(8,128)(2,1)}, u32[]{:S(2)}) copy-start(bf16[1024,128]{1,0:T(8,128)(2,1)} %param.14) | copy-start | bytes 786436
  215.5 3.5 %copy-start.4 = (bf16[8,256,1024]{2,1,0:T(8,128)(2,1)S(1)}, bf16[8,256,1024]{2,1,0:T(8,128)(2,1)}, u32[]{:S(2)}) copy-start(bf16[8,256,1024]{2,1,0:T(8,128)(2,1)} %all-gather.8.cloned.1.call-done) | copy-start | bytes 12582916
Sparse Core Ops, SparseCore 0:
  72.6 56.0 all-gather.5
  130.9 42.6 all-gather.3
  175.1 33.2 all-gather.7

commit v3 on v2

--- a/solution.py
+++ b/solution.py
@@ -23,65 +23,195 @@
     return hashed
 
 
-def table_kernel(cols, base_ref, out_ref):
-    rows, width = out_ref.shape
-    step, piece = 16, 512
-    base = base_ref[pl.program_id(0)] + pl.program_id(1) * width
-    local = lax.broadcasted_iota(jnp.int32, (step, piece), 0) * cols + lax.broadcasted_iota(
-        jnp.int32, (step, piece), 1
-    )
-
-    def one(i, carry):
-        for j in range(width // piece):
-            h = local + (base + i * (step * cols) + j * piece)
-            h = h ^ lax.shift_right_logical(h, jnp.int32(16))
-            h = h * jnp.int32(M1)
-            h = h ^ lax.shift_right_logical(h, jnp.int32(15))
-            h = h * jnp.int32(M2_UP)
-            h = h ^ lax.shift_left(h, jnp.int32(16))
-            sign = jnp.where(h < 0, jnp.float32(-1.0), jnp.float32(1.0))
-            out_ref[pl.ds(pl.multiple_of(i * step, step), step), j * piece : (j + 1) * piece] = (
-                sign.astype(jnp.bfloat16)
+CHUNKS = 4
+TABLE_ROWS = 64
+
+
+def front_kernel(
+    shards, cols,
+    base_ref, in_ref, gr_ref, low_in_ref, low_gr_ref, table_ref,
+    pair, mine, land, full, block, sends, recvs, sends_z, recvs_z, sends_g, recvs_g, sends_x, recvs_x,
+    store,
+):
+    me = lax.axis_index("proj")
+    rest = shards // 2
+    x, z = lax.rem(me, 2), me // 2
+    rows = in_ref.shape[0] // 2
+    half = rows // 2
+    piece = half // rest
+    parts = [in_ref, gr_ref]
+    partner = z * 2 + (1 - x)
+    others = [lax.rem(z + d, rest) for d in range(1, rest)]
+
+    barrier = pltpu.get_barrier_semaphore()
+    for target in [partner] + [o * 2 + x for o in others]:
+        pl.semaphore_signal(
+            barrier, inc=1, device_id={"proj": target}, device_id_type=pl.DeviceIdType.MESH
+        )
+    pl.semaphore_wait(barrier, rest)
+
+    def remote(src, dst, send, recv, target):
+        return pltpu.make_async_remote_copy(
+            src_ref=src, dst_ref=dst, send_sem=send, recv_sem=recv,
+            device_id={"proj": target}, device_id_type=pl.DeviceIdType.MESH,
+        )
+
+    def span(start, size):
+        return pl.ds(pl.multiple_of(start, 16), size)
+
+    one, two, three, four = {}, {}, {}, {}
+    for c in range(CHUNKS):
+        r0 = (c % 2) * rows
+        one[c] = remote(
+            parts[c // 2].at[span(r0 + (1 - x) * half, half)], pair.at[c],
+            sends.at[c], recvs.at[c], partner,
+        )
+        one[c].start()
+
+    def stage1(c):
+        r0 = (c % 2) * rows
+        one[c].wait_recv()
+        mine[c] = (
+            parts[c // 2][span(r0 + x * half, half), :].astype(jnp.float32)
+            + pair[c].astype(jnp.float32)
+        ).astype(jnp.bfloat16)
+        two[c] = []
+        for d in range(1, rest):
+            s = c * (rest - 1) + d - 1
+            copy = remote(
+                mine.at[c, span(others[d - 1] * piece, piece)], land.at[s],
+                sends_z.at[s], recvs_z.at[s], others[d - 1] * 2 + x,
             )
+            copy.start()
+            two[c].append(copy)
+
+    def stage2(c):
+        total = mine[c, span(z * piece, piece), :].astype(jnp.float32)
+        for copy in two[c]:
+            copy.wait_recv()
+        for d in range(1, rest):
+            total = total + land[c * (rest - 1) + d - 1].astype(jnp.float32)
+        where = span((c % 2) * rows + x * half + z * piece, piece)
+        full[c // 2, where, :] = (UPDATE_MULTIPLIER * total).astype(jnp.bfloat16)
+        three[c] = []
+        for d in range(1, rest):
+            s = c * (rest - 1) + d - 1
+            copy = remote(
+                full.at[c // 2, where], full.at[c // 2, where],
+                sends_g.at[s], recvs_g.at[s], others[d - 1] * 2 + x,
+            )
+            copy.start()
+            three[c].append(copy)
+
+    def stage3(c):
+        for copy in three[c]:
+            copy.wait_recv()
+        where = span((c % 2) * rows + x * half, half)
+        four[c] = remote(
+            full.at[c // 2, where], full.at[c // 2, where], sends_x.at[c], recvs_x.at[c], partner
+        )
+        four[c].start()
+
+    blocks = table_ref.shape[0] // TABLE_ROWS
+    step, wide = 16, 512
+    local = lax.broadcasted_iota(jnp.int32, (step, wide), 0) * cols + lax.broadcasted_iota(
+        jnp.int32, (step, wide), 1
+    )
+    per_tile = 128 // TABLE_ROWS
+
+    def stored(b):
+        slot = lax.rem(b, 2)
+        return pltpu.make_async_copy(
+            block.at[slot],
+            table_ref.at[pl.ds(pl.multiple_of(b * TABLE_ROWS, TABLE_ROWS), TABLE_ROWS)],
+            store.at[slot],
+        )
+
+    def table_block(b, carry):
+        slot = lax.rem(b, 2)
+
+        @pl.when(b >= 2)
+        def _():
+            stored(b - 2).wait()
+
+        base = base_ref[b // per_tile] + lax.rem(b, per_tile) * (TABLE_ROWS * cols)
+
+        def piece_rows(i, inner):
+            row = lax.rem(i, TABLE_ROWS // step) * step
+            left = (i // (TABLE_ROWS // step)) * (4 * wide)
+            for j in range(4):
+                h = local + (base + row * cols + left + j * wide)
+                h = h ^ lax.shift_right_logical(h, jnp.int32(16))
+                h = h * jnp.int32(M1)
+                h = h ^ lax.shift_right_logical(h, jnp.int32(15))
+                h = h * jnp.int32(M2_UP)
+                h = h ^ lax.shift_left(h, jnp.int32(16))
+                sign = jnp.where(h < 0, jnp.float32(-1.0), jnp.float32(1.0))
+                block[
+                    slot,
+                    pl.ds(pl.multiple_of(row, step), step),
+                    pl.ds(pl.multiple_of(left + j * wide, wide), wide),
+                ] = sign.astype(jnp.bfloat16)
+            return inner
+
+        lax.fori_loop(0, (TABLE_ROWS // step) * (cols // (4 * wide)), piece_rows, 0)
+        stored(b).start()
         return carry
 
-    lax.fori_loop(0, rows // step, one, 0)
-
-
-def sign_tables(bases, cols):
-    blocks = bases.shape[0]
-    width = 2048
+    plan = [
+        [],
+        [(stage1, 0)],
+        [(stage1, 1)],
+        [(stage2, 0), (stage1, 2)],
+        [(stage2, 1), (stage1, 3)],
+        [(stage3, 0), (stage2, 2)],
+        [(stage3, 1), (stage2, 3), (stage3, 2), (stage3, 3)],
+    ]
+    ticks = len(plan) - 1
+    for t, jobs in enumerate(plan):
+        for job, c in jobs:
+            job(c)
+        if t < ticks:
+            lax.fori_loop(blocks * t // ticks, blocks * (t + 1) // ticks, table_block, 0)
+    for c in range(CHUNKS):
+        four[c].wait_recv()
+    low_in_ref[...] = full[0]
+    low_gr_ref[...] = full[1]
+    stored(blocks - 2).wait()
+    stored(blocks - 1).wait()
+    for c in range(CHUNKS):
+        for copy in [one[c], four[c]] + two[c] + three[c]:
+            copy.wait_send()
+
+
+def front(bases, part_in, part_gr, shards, cols):
+    total, rank = part_in.shape
+    rest = shards // 2
+    half = total // 4
+    vmem = pl.BlockSpec(memory_space=pltpu.VMEM)
+    sems = [pltpu.SemaphoreType.DMA((CHUNKS,))] * 2
+    many = [pltpu.SemaphoreType.DMA((CHUNKS * (rest - 1),))] * 4
     return pl.pallas_call(
-        functools.partial(table_kernel, cols),
-        grid=(blocks, cols // width),
-        in_specs=[pl.BlockSpec(memory_space=pltpu.SMEM)],
-        out_specs=pl.BlockSpec((128, width), lambda i, j: (i, j)),
-        out_shape=jax.ShapeDtypeStruct((blocks * 128, cols), jnp.bfloat16),
-        cost_estimate=pl.CostEstimate(
-            flops=blocks * 128 * cols * 12, bytes_accessed=blocks * 256 * cols, transcendentals=0
+        functools.partial(front_kernel, shards, cols),
+        in_specs=[pl.BlockSpec(memory_space=pltpu.SMEM), vmem, vmem],
+        out_specs=[vmem, vmem, pl.BlockSpec(memory_space=pl.ANY)],
+        out_shape=[
+            jax.ShapeDtypeStruct((total, rank), jnp.bfloat16),
+            jax.ShapeDtypeStruct((total, rank), jnp.bfloat16),
+            jax.ShapeDtypeStruct((bases.shape[0] * 128, cols), jnp.bfloat16),
+        ],
+        scratch_shapes=[
+            pltpu.VMEM((CHUNKS, half, rank), jnp.bfloat16),
+            pltpu.VMEM((CHUNKS, half, rank), jnp.bfloat16),
+            pltpu.VMEM((CHUNKS * (rest - 1), half // rest, rank), jnp.bfloat16),
+            pltpu.VMEM((2, total, rank), jnp.bfloat16),
+            pltpu.VMEM((2, TABLE_ROWS, cols), jnp.bfloat16),
+        ] + sems + many + sems + [pltpu.SemaphoreType.DMA((2,))],
+        compiler_params=pltpu.CompilerParams(
+            collective_id=1, has_side_effects=True, vmem_limit_bytes=40 * 1024 * 1024
         ),
-        name="sign_tables",
-    )(bases)
-
-
-def share_kernel(pieces_ref, order_ref, out_ref):
-    total = pieces_ref[0].astype(jnp.float32)
-    for i in range(1, pieces_ref.shape[0]):
-        total = total + pieces_ref[i].astype(jnp.float32)
-    out_ref[...] = (UPDATE_MULTIPLIER * total).astype(jnp.bfloat16)
-
-
-def share_of(pieces, after, name):
-    _, rows, rank = pieces.shape
-    vmem = pl.BlockSpec(memory_space=pltpu.VMEM)
-    return pl.pallas_call(
-        share_kernel,
-        in_specs=[vmem, pl.BlockSpec(memory_space=pl.ANY)],
-        out_specs=vmem,
-        out_shape=jax.ShapeDtypeStruct((rows, rank), jnp.bfloat16),
-        compiler_params=pltpu.CompilerParams(vmem_limit_bytes=16 * 1024 * 1024),
-        name=name,
-    )(pieces, after)
+        name="front",
+    )(bases, part_in, part_gr)
 
 
 def step_kernel(wide_ref, low_ref, moment_ref, second_ref, order_ref, out_ref):
@@ -132,18 +262,18 @@
         out_ref[i : i + 1, :] = row
 
 
-def project(step, tables, name, prior):
+def project(step, tables, which, name, prior):
     rows, w = step.shape
     n = rows // RANK
     cols = tables.shape[1]
     tile = min(512, w)
     inner = w // tile
-    edge = w // RANK
+    edge = 2 * w // RANK
     out = pl.BlockSpec((None, n, tile), lambda k: (k // inner, 0, k % inner))
     in_specs = [
         pl.BlockSpec((rows, w), lambda k: (0, 0)),
-        pl.BlockSpec((w, tile), lambda k: (0, k)),
-        pl.BlockSpec((RANK, tile), lambda k: (edge, k)),
+        pl.BlockSpec((w, tile), lambda k: (which, k)),
+        pl.BlockSpec((RANK, tile), lambda k: (edge + which, k)),
     ]
     operands = [step, tables, tables]
     if prior is not None:
@@ -290,35 +420,30 @@
         preferred_element_type=jnp.float32,
     ).astype(jnp.bfloat16)
 
-    def pieces_of(part):
-        return lax.all_to_all(
-            part.reshape(shards, n * tok // shards, RANK), "proj", split_axis=0, concat_axis=0
-        )
-
-    def gather(share):
-        return lax.all_gather(share, "proj", axis=0, tiled=True).reshape(n, tok, RANK)
-
     seed4 = sketch_random_key[0] * 4
     inner = jnp.arange(w // RANK, dtype=jnp.int32) * (RANK * K) + shard_id * (w * K)
-    tables = [
-        sign_tables(
-            jnp.concatenate([scramble(seed4 + wide) + inner, scramble(seed4 + narrow)[None]]), K
-        )
-        for wide, narrow in ((1, 0), (2, 3))
-    ]
-    low_in = gather(share_of(pieces_of(part_in), tables[0], "share_in"))
-    low_gr = gather(share_of(pieces_of(part_gr), tables[1], "share_gr"))
+    bases = jnp.concatenate([
+        scramble(seed4 + 1) + inner,
+        scramble(seed4 + 2) + inner,
+        scramble(seed4)[None],
+        scramble(seed4 + 3)[None],
+    ])
+    low_in, low_gr, tables = front(
+        bases, part_in.reshape(n * tok, RANK), part_gr.reshape(n * tok, RANK), shards, K
+    )
+    low_in = low_in.reshape(n, tok, RANK)
+    low_gr = low_gr.reshape(n, tok, RANK)
 
     up = steps(
-        loss_slope_at_result, low_in, mean_estimate_right, variance_estimate_right, tables[1],
+        loss_slope_at_result, low_in, mean_estimate_right, variance_estimate_right, tables,
         "steps_up"
     )
-    half = project(up, tables[0], "project_up", None)
+    half = project(up, tables, 0, "project_up", None)
     dn = steps(
         mapped_layer_arguments, low_gr, mean_estimate_left.T, variance_estimate_left.T, half,
         "steps_down"
     )
-    projected = project(dn, tables[1], "project_down", half)
+    projected = project(dn, tables, 1, "project_down", half)
 
     all_val = lax.all_gather(heldout_sketched_slopes, "lang", axis=0, tiled=True)
     val_wide = all_val.astype(jnp.float32)

time: 252 us -> 240 us (0.952)
  Pallas kernels: 145 us -> 194 us
  waiting for transfers between devices: 26.3 us -> 0.7 us
  local copies, waits for them, and re-layouts: 30.9 us -> 9.57 us
  starting transfers between devices: 11.2 us -> 0.04 us
    pallas_call x4 -> x1, Pallas kernels: 49.1 us -> 93.6 us  [front(): pl.pallas_call(functools.partial(front_kernel, shards, cols), in_specs=[p...]
    unnamed x31 -> x43, local copies, waits for them, and re-layouts: 30.1 us -> 8.85 us
    all_to_all x2 -> x0, waiting for transfers between devices: 14.7 us -> none  [pieces_of(): lax.all_to_all(part.reshape(shards, n * tok // shards, RANK), 'proj', spl...]
    all_gather x2 -> x0, waiting for transfers between devices: 11 us -> none  [gather(): lax.all_gather(share, 'proj', axis=0, tiled=True).reshape(n, tok, RANK)]
    all_to_all x2 -> x0, starting transfers between devices: 10.9 us -> none  [pieces_of(): lax.all_to_all(part.reshape(shards, n * tok // shards, RANK), 'proj', spl...]
    pallas_call x1, Pallas kernels: 24.2 us -> 28.7 us  [finish(): pl.pallas_call(functools.partial(finish_kernel, shards, langs, nval), in_...]
  transfers between devices with their start and end apart: 5 -> 1, of which waited for: 4 -> 0; matrix products, arithmetic and copies ran while one was open for 5% -> 8% of each run, Pallas kernels for 48% -> 69%
where the time goes in v3:
time: 240 us
  Pallas kernels  194 us (81%)
  matrix products  17 us (7%)
  between operations  15 us (6%)
  local copies, waits for them, and re-layouts  9.57 us (4%)
  other arithmetic  3.66 us (2%)
    pallas_call x1, Pallas kernels, front(): pl.pallas_call(functools.partial(front_kernel, shards, cols), in_specs=[p...  93.6 us
    pallas_call x2, Pallas kernels, project(): pl.pallas_call(functools.partial(project_kernel, prior is not None), grid...  62 us
    pallas_call x1, Pallas kernels, finish(): pl.pallas_call(functools.partial(finish_kernel, shards, langs, nval), in_...  28.7 us
    pallas_call x2, Pallas kernels, steps(): pl.pallas_call(step_kernel, grid=(n,), in_specs=[pl.BlockSpec((1, tok, w)...  9.63 us
    dot_general x1, matrix products, per_device(): jnp.einsum('ntw,rw->ntr', loss_slope_at_result, right_lowrank_weights, pr...  8.95 us
    unnamed x43, local copies, waits for them, and re-layouts  8.85 us
    dot_general x1, matrix products, per_device(): jnp.einsum('ntw,wr->ntr', mapped_layer_arguments, left_lowrank_weights, p...  8.09 us
  transfers between devices with their start and end apart: 1, of which 0 were waited for; matrix products, arithmetic and copies ran while one was open for 8% of the time, Pallas kernels for 69%

profile of v3, /device:TPU:0, one launch (start us, length us, event | category | flops | bytes accessed | tf_op | source)
XLA Modules:
  0.0 239.9 jit_solution(5825770858719424996)
XLA Ops:
  7.2 0.0 copy-start
  7.2 0.0 all-gather.2.cloned.1.call-start
  7.2 0.7 all-gather.2.cloned.1.call-update
  8.6 0.0 copy-done
  8.6 0.0 copy-start.11
  8.6 0.0 copy-start.13
  8.6 0.0 copy-start.10
  8.6 0.0 copy-start.12
  8.6 8.1 %convolution_convert_fusion.1 = bf16[12,512,128]{2,1,0:T(8,128)(2,1)S(1)} fusion(bf16[12,512,1024]{2,1,0:T(8,128)(2,1)} %wide_ref.3, bf16[1024,128]{1,0:T(8,128)(2,1)S(1)} %copy-done), kind=kOutput, calls=%fused_computation.2 | convolution fusion | flops 1611399168 | bytes 14417920 | tf_op jit(solution)/shard_map/ntw,wr->ntr/dot_general | solution.py:414
  16.7 0.0 copy-done.11
  16.7 0.0 copy-done.13
  16.7 0.2 multiply_reduce_fusion.2
  16.9 0.0 copy-done.10
  17.0 0.2 copy.23
  17.2 2.1 copy.24
  19.3 0.1 copy.25.count_ref
  19.4 0.0 slice-start.3
  19.4 0.1 pad_add_fusion.base_ref
  19.4 0.0 copy-done.12
  19.4 0.0 slice-start.4
  19.4 0.0 slice-start.5
  19.4 8.9 %convolution_convert_fusion = bf16[12,512,128]{2,1,0:T(8,128)(2,1)S(1)} fusion(bf16[12,512,1024]{2,1,0:T(8,128)(2,1)} %wide_ref.2, bf16[128,1024]{1,0:T(8,128)(2,1)S(1)} %copy-done.12), kind=kOutput, calls=%fused_computation.1 | convolution fusion | flops 1611399168 | bytes 14417920 | tf_op jit(solution)/shard_map/ntw,rw->ntr/dot_general | solution.py:418
  28.4 93.6 %front.1 = (bf16[6144,128]{1,0:T(8,128)(2,1)S(1)}, bf16[6144,128]{1,0:T(8,128)(2,1)S(1)}, bf16[2304,8192]{1,0:T(8,128)(2,1)}) custom-call(s32[18]{0:T(128)S(1)} %pad_add_fusion.base_ref, bf16[6144,128]{1,0:T(8,128)(2,1)S(1)} %bitcast.29, bf16[6144,128]{1,0:T(8,128)(2,1)S(1)} %bitcast.30), custom_call_target="tpu_custom_call" | custom-call | tf_op jit(solution)/shard_map/front/pallas_call | solution.py:194
  122.0 0.0 copy-start.4
  122.0 1.1 copy-done.4
  123.1 0.0 copy-start.6
  123.1 1.2 copy-done.6
  124.2 0.0 slice-done.3
  124.2 0.0 slice-done.4
  124.2 0.0 slice-done.5
  124.2 0.0 copy-start.5
  124.2 1.4 copy-done.5
  125.7 0.0 copy-start.8
  125.7 1.0 copy-done.8
  126.7 0.0 copy-start.9
  126.7 1.0 copy-done.9
  127.7 0.0 slice-start
  127.7 0.0 slice-start.1
  127.7 4.8 %steps_up.1.refs_0_ = bf16[1536,1024]{1,0:T(8,128)(2,1)S(1)} custom-call(bf16[12,512,1024]{2,1,0:T(8,128)(2,1)S(1)} %bitcast.24, bf16[12,512,128]{2,1,0:T(8,128)(2,1)S(1)} %bitcast.27, f32[128,1024]{1,0:T(8,128)S(1)} %copy-done.8, f32[128,1024]{1,0:T(8,128)S(1)} %copy-done.9, bf16[2304,8192]{1,0:T(8,128)(2,1)} %get-tuple-element.9.order_ref.refs_1_.refs_2_), custom_call_target="tpu_custom_call" | custom-call | flops 1610612736 | bytes 12582912 | tf_op jit(solution)/shard_map/steps_up/pallas_call | solution.py:230
  132.6 0.0 slice-start.2
  132.6 0.0 copy-start.3
  132.6 0.0 copy-start.7
  132.6 31.0 %project_up.1.order_ref.refs_3_ = f32[8,12,1024]{2,1,0:T(8,128)S(1)} custom-call(bf16[1536,1024]{1,0:T(8,128)(2,1)S(1)} %steps_up.1.refs_0_, bf16[2304,8192]{1,0:T(8,128)(2,1)} %get-tuple-element.9.order_ref.refs_1_.refs_2_, bf16[2304,8192]{1,0:T(8,128)(2,1)} %get-tuple-element.9.order_ref.refs_1_.refs_2_), custom_call_target="tpu_custom_call" | custom-call | flops 25769803776 | bytes 19922944 | tf_op jit(solution)/shard_map/project_up/pallas_call | solution.py:282
  163.6 0.0 slice-done
  163.6 0.0 slice-done.1
  163.6 0.0 slice-done.2
  163.6 0.0 copy-done.3
  163.6 0.0 copy-done.7
  163.6 4.8 %steps_down.1.refs_0_ = bf16[1536,1024]{1,0:T(8,128)(2,1)S(1)} custom-call(bf16[12,512,1024]{2,1,0:T(8,128)(2,1)S(1)} %bitcast.22, bf16[12,512,128]{2,1,0:T(8,128)(2,1)S(1)} %bitcast.28, f32[128,1024]{1,0:T(8,128)S(1)} %bitcast.25, f32[128,1024]{1,0:T(8,128)S(1)} %bitcast.26, f32[8,12,1024]{2,1,0:T(8,128)S(1)} %project_up.1.order_ref.refs_3_), custom_call_target="tpu_custom_call" | custom-call | flops 1610612736 | bytes 12582912 | tf_op jit(solution)/shard_map/steps_down/pallas_call | solution.py:230
  168.5 0.1 fusion.2.hot_ref
  168.5 0.0 copy-start.1
  168.5 31.0 %project_down.1.proj_ref = f32[8,12,1024]{2,1,0:T(8,128)S(1)} custom-call(bf16[1536,1024]{1,0:T(8,128)(2,1)S(1)} %steps_down.1.refs_0_, bf16[2304,8192]{1,0:T(8,128)(2,1)} %get-tuple-element.9.order_ref.refs_1_.refs_2_, bf16[2304,8192]{1,0:T(8,128)(2,1)} %get-tuple-element.9.order_ref.refs_1_.refs_2_, f32[8,12,1024]{2,1,0:T(8,128)S(1)} %project_up.1.order_ref.refs_3_), custom_call_target="tpu_custom_call" | custom-call | flops 25769803776 | bytes 19922944 | tf_op jit(solution)/shard_map/project_down/pallas_call | solution.py:282
  199.6 0.0 all-gather.2.cloned.1.call-done
  199.6 0.0 copy-start.2
  199.6 3.2 %multiply_reduce_fusion = f32[8,256]{1,0:T(8,128)S(1)} fusion(bf16[8,256,1024]{2,1,0:T(8,128)(2,1)} %all-gather.2.cloned.1.call-done), kind=kLoop, calls=%fused_computation | loop fusion | flops 6289408 | bytes 4202496 | tf_op jit(solution)/shard_map/reduce_sum | solution.py:450
  202.9 0.1 multiply_reduce_fusion.1.square_ref
  203.0 0.1 copy-done.2
  203.1 28.7 %finish.1 = (f32[12,1024]{1,0:T(8,128)S(1)}, f32[12,128]{1,0:T(8,128)S(1)}) custom-call(f32[8,12,1024]{2,1,0:T(8,128)S(1)} %project_down.1.proj_ref, bf16[2048,1024]{1,0:T(8,128)(2,1)S(1)} %bitcast.20, f32[12,8]{1,0:T(8,128)S(1)} %fusion.2.hot_ref, f32[12,256]{1,0:T(8,128)S(1)} %multiply_reduce_fusion.1.square_ref, s32[12,1]{1,0:T(8,128)S(1)} %copy.25.count_ref), custom_call_target="tpu_custom_call" | custom-call | tf_op jit(solution)/shard_map/finish/pallas_call | solution.py:371
  231.8 0.6 slice_reduce_fusion
  232.4 0.6 copy.28
  233.0 0.0 copy-done.1
  (3 shorter events, 0.0 us)
Async XLA Ops:
  7.2 1.4 copy-start
  7.2 192.4 %all-gather.2.cloned.1.call-start = ((), (), s32[]{:S(2)}) async-start(), calls=%async_computation | async-start | bytes 5242880 | tf_op jit(solution)/shard_map/all_gather | solution.py:448
  8.6 8.1 %copy-start.11 = (s32[12,1]{0,1:T(1,128)S(1)}, s32[12,1]{0,1:T(1,128)}, u32[]{:S(2)}) copy-start(s32[12,1]{0,1:T(1,128)} %param.21) | copy-start | bytes 148
  8.6 8.1 %copy-start.13 = (s32[8]{0:T(128)S(1)}, s32[8]{0:T(128)}, u32[]{:S(2)}) copy-start(s32[8]{0:T(128)} %param.22) | copy-start | bytes 100
  8.6 8.3 %copy-start.10 = (f32[1024,128]{1,0:T(8,128)S(1)}, f32[1024,128]{1,0:T(8,128)}, u32[]{:S(2)}) copy-start(f32[1024,128]{1,0:T(8,128)} %param.16) | copy-start | bytes 1572868
  8.6 10.8 %copy-start.12 = (bf16[128,1024]{1,0:T(8,128)(2,1)S(1)}, bf16[128,1024]{1,0:T(8,128)(2,1)}, u32[]{:S(2)}) copy-start(bf16[128,1024]{1,0:T(8,128)(2,1)} %param.15) | copy-start | bytes 786436
  19.4 104.9 %slice-start.3 = ((s8[12582912]{0:T(1024)(128)(4,1)}), s8[4194304]{0:T(1024)(128)(4,1)S(1)}, s32[]{:S(2)}) async-start(s8[12582912]{0:T(1024)(128)(4,1)} %bitcast.23), calls=%async_computation.4 | async-start | bytes 8388608
  19.4 104.8 %slice-start.4 = ((s8[12582912]{0:T(1024)(128)(4,1)}), s8[4194304]{0:T(1024)(128)(4,1)S(1)}, s32[]{:S(2)}) async-start(s8[12582912]{0:T(1024)(128)(4,1)} %bitcast.23), calls=%async_computation.5 | async-start | bytes 8388608
  19.4 104.8 %slice-start.5 = ((s8[12582912]{0:T(1024)(128)(4,1)}), s8[4194304]{0:T(1024)(128)(4,1)S(1)}, s32[]{:S(2)}) async-start(s8[12582912]{0:T(1024)(128)(4,1)} %bitcast.23), calls=%async_computation.6 | async-start | bytes 8388608
  122.0 1.1 copy-start.4
  123.1 1.2 copy-start.6
  124.2 1.4 copy-start.5
  125.7 1.0 copy-start.8
  126.7 1.0 copy-start.9
  127.7 35.8 %slice-start = ((s8[12582912]{0:T(1024)(128)(4,1)}), s8[4194304]{0:T(1024)(128)(4,1)S(1)}, s32[]{:S(2)}) async-start(s8[12582912]{0:T(1024)(128)(4,1)} %bitcast.21), calls=%async_computation.1 | async-start | bytes 8388608
  127.7 35.8 %slice-start.1 = ((s8[12582912]{0:T(1024)(128)(4,1)}), s8[4194304]{0:T(1024)(128)(4,1)S(1)}, s32[]{:S(2)}) async-start(s8[12582912]{0:T(1024)(128)(4,1)} %bitcast.21), calls=%async_computation.2 | async-start | bytes 8388608
  132.6 31.0 %slice-start.2 = ((s8[12582912]{0:T(1024)(128)(4,1)}), s8[4194304]{0:T(1024)(128)(4,1)S(1)}, s32[]{:S(2)}) async-start(s8[12582912]{0:T(1024)(128)(4,1)} %bitcast.21), calls=%async_computation.3 | async-start | bytes 8388608
  132.6 31.0 %copy-start.3 = (f32[1024,128]{0,1:T(8,128)S(1)}, f32[1024,128]{0,1:T(8,128)}, u32[]{:S(2)}) copy-start(f32[1024,128]{0,1:T(8,128)} %copy.24) | copy-start | bytes 1572868
  132.6 31.0 %copy-start.7 = (bf16[6144,128]{1,0:T(8,128)(2,1)S(1)}, bf16[6144,128]{1,0:T(8,128)(2,1)}, u32[]{:S(2)}) copy-start(bf16[6144,128]{1,0:T(8,128)(2,1)} %copy-done.6) | copy-start | bytes 4718596
  168.5 64.5 %copy-start.1 = (bf16[1024,128]{1,0:T(8,128)(2,1)S(1)}, bf16[1024,128]{1,0:T(8,128)(2,1)}, u32[]{:S(2)}) copy-start(bf16[1024,128]{1,0:T(8,128)(2,1)} %param.14) | copy-start | bytes 786436
  199.6 3.5 %copy-start.2 = (bf16[8,256,1024]{2,1,0:T(8,128)(2,1)S(1)}, bf16[8,256,1024]{2,1,0:T(8,128)(2,1)}, u32[]{:S(2)}) copy-start(bf16[8,256,1024]{2,1,0:T(8,128)(2,1)} %all-gather.2.cloned.1.call-done) | copy-start | bytes 12582916
Sparse Core Ops, SparseCore 0:
  9.6 37.1 all-gather.1

commit v4 on v3

--- a/solution.py
+++ b/solution.py
@@ -208,7 +208,7 @@
             pltpu.VMEM((2, TABLE_ROWS, cols), jnp.bfloat16),
         ] + sems + many + sems + [pltpu.SemaphoreType.DMA((2,))],
         compiler_params=pltpu.CompilerParams(
-            collective_id=1, has_side_effects=True, vmem_limit_bytes=40 * 1024 * 1024
+            collective_id=1, has_side_effects=True, vmem_limit_bytes=24 * 1024 * 1024
         ),
         name="front",
     )(bases, part_in, part_gr)
@@ -320,8 +320,8 @@
         )
         copy.start()
         first.append(copy)
-    message[n:, :] = jnp.zeros((message.shape[0] - n, message.shape[1]), jnp.float32)
-    message[16 : 16 + n, :nval] = square_ref[...]
+    message[...] = jnp.zeros(message.shape, jnp.bfloat16)
+    message[16 : 16 + n, :nval] = square_ref[...].astype(jnp.bfloat16)
     raw = proj_ref[me]
     for copy in first:
         copy.wait_recv()
@@ -334,10 +334,10 @@
     own = jnp.zeros((n, nval), jnp.float32)
     for l in range(langs):
         own = own + hot_ref[:, l : l + 1] * dots[:, l * nval : (l + 1) * nval]
-    message[:n, :nval] = own
+    message[:n, :nval] = own.astype(jnp.bfloat16)
     message[:n, nval:] = jnp.broadcast_to(
         jnp.sum(raw * raw, axis=1, keepdims=True), (n, message.shape[1] - nval)
-    )
+    ).astype(jnp.bfloat16)
     second = []
     for d in range(1, shards):
         target = lax.rem(me + d, shards)
@@ -348,11 +348,11 @@
         )
         copy.start()
         second.append(copy)
-    total = message[...]
+    total = message[...].astype(jnp.float32)
     for copy in second:
         copy.wait_recv()
     for d in range(1, shards):
-        total = total + notes[d - 1]
+        total = total + notes[d - 1].astype(jnp.float32)
     inverse = lax.rsqrt(total[:n, nval : nval + 1] / cols + 1e-06)
     feat_ref[...] = raw * inverse
     rms = jnp.sqrt(total[16 : 16 + n, :nval] / cols + 1e-06)
@@ -378,8 +378,8 @@
         ],
         scratch_shapes=[
             pltpu.VMEM((shards - 1, n, w), jnp.float32),
-            pltpu.VMEM((32, nval + 128), jnp.float32),
-            pltpu.VMEM((shards - 1, 32, nval + 128), jnp.float32),
+            pltpu.VMEM((32, nval + 128), jnp.bfloat16),
+            pltpu.VMEM((shards - 1, 32, nval + 128), jnp.bfloat16),
             pltpu.SemaphoreType.DMA((shards - 1,)),
             pltpu.SemaphoreType.DMA((shards - 1,)),
             pltpu.SemaphoreType.DMA((shards - 1,)),

time: 240 us -> 232 us (0.967)
  local copies, waits for them, and re-layouts: 9.57 us -> 3.92 us
    unnamed x43 -> x39, local copies, waits for them, and re-layouts: 8.85 us -> 3.2 us
  transfers between devices with their start and end apart: 1 -> 1, of which waited for: 0 -> 0; matrix products, arithmetic and copies ran while one was open for 8% -> 8% of each run, Pallas kernels for 69% -> 70%
where the time goes in v4:
time: 232 us
  Pallas kernels  192 us (83%)
  matrix products  17.3 us (7%)
  between operations  15 us (6%)
  local copies, waits for them, and re-layouts  3.92 us (2%)
  other arithmetic  3.66 us (2%)
    pallas_call x1, Pallas kernels, front(): pl.pallas_call(functools.partial(front_kernel, shards, cols), in_specs=[p...  91.9 us
    pallas_call x2, Pallas kernels, project(): pl.pallas_call(functools.partial(project_kernel, prior is not None), grid...  62.1 us
    pallas_call x1, Pallas kernels, finish(): pl.pallas_call(functools.partial(finish_kernel, shards, langs, nval), in_...  27.9 us
    pallas_call x2, Pallas kernels, steps(): pl.pallas_call(step_kernel, grid=(n,), in_specs=[pl.BlockSpec((1, tok, w)...  9.7 us
    dot_general x1, matrix products, per_device(): jnp.einsum('ntw,rw->ntr', loss_slope_at_result, right_lowrank_weights, pr...  9.24 us
    dot_general x1, matrix products, per_device(): jnp.einsum('ntw,wr->ntr', mapped_layer_arguments, left_lowrank_weights, p...  8.1 us
  transfers between devices with their start and end apart: 1, of which 0 were waited for; matrix products, arithmetic and copies ran while one was open for 8% of the time, Pallas kernels for 70%

profile of v4, /device:TPU:0, one launch (start us, length us, event | category | flops | bytes accessed | tf_op | source)
XLA Modules:
  0.0 232.3 jit_solution(531017488121051686)
XLA Ops:
  7.2 0.0 copy-start
  7.2 0.0 all-gather.2.cloned.1.call-start
  7.2 0.7 all-gather.2.cloned.1.call-update
  8.6 0.0 copy-done
  8.6 0.0 copy-start.10
  8.6 0.0 copy-start.11
  8.6 0.0 copy-start.8
  8.6 0.0 copy-start.9
  8.6 8.1 %convolution_convert_fusion.1 = bf16[12,512,128]{2,1,0:T(8,128)(2,1)S(1)} fusion(bf16[12,512,1024]{2,1,0:T(8,128)(2,1)} %wide_ref.3, bf16[1024,128]{1,0:T(8,128)(2,1)S(1)} %copy-done), kind=kOutput, calls=%fused_computation.2 | convolution fusion | flops 1611399168 | bytes 14417920 | tf_op jit(solution)/shard_map/ntw,wr->ntr/dot_general | solution.py:414
  16.7 0.0 copy-done.10
  16.7 0.0 copy-done.11
  16.7 0.2 multiply_reduce_fusion.2
  17.0 0.0 copy-done.8
  17.0 0.2 copy.23
  17.2 0.0 copy-done.9
  17.2 1.0 copy.24
  18.2 0.1 copy.25.count_ref
  18.3 0.0 slice-start.3
  18.3 0.1 pad_add_fusion.base_ref
  18.4 0.0 slice-start.4
  18.4 0.0 slice-start.5
  18.4 0.0 copy-start.6
  18.4 0.0 copy-start.7
  18.4 9.2 %convolution_convert_fusion = bf16[12,512,128]{2,1,0:T(8,128)(2,1)S(1)} fusion(bf16[12,512,1024]{2,1,0:T(8,128)(2,1)} %wide_ref.2, bf16[128,1024]{1,0:T(8,128)(2,1)} %param.15), kind=kOutput, calls=%fused_computation.1 | convolution fusion | flops 1611399168 | bytes 14417920 | tf_op jit(solution)/shard_map/ntw,rw->ntr/dot_general | solution.py:418
  27.6 91.9 %front.1 = (bf16[6144,128]{1,0:T(8,128)(2,1)S(1)}, bf16[6144,128]{1,0:T(8,128)(2,1)S(1)}, bf16[2304,8192]{1,0:T(8,128)(2,1)}) custom-call(s32[18]{0:T(128)S(1)} %pad_add_fusion.base_ref, bf16[6144,128]{1,0:T(8,128)(2,1)S(1)} %bitcast.29, bf16[6144,128]{1,0:T(8,128)(2,1)S(1)} %bitcast.30), custom_call_target="tpu_custom_call" | custom-call | tf_op jit(solution)/shard_map/front/pallas_call | solution.py:194
  119.5 0.0 copy-start.4
  119.6 1.2 copy-done.4
  120.7 0.0 slice-done.3
  120.7 0.0 slice-done.4
  120.7 0.0 slice-done.5
  120.7 0.0 copy-done.6
  120.7 0.0 copy-done.7
  120.7 0.0 slice-start
  120.8 0.0 slice-start.1
  120.8 4.8 %steps_up.1.refs_0_ = bf16[1536,1024]{1,0:T(8,128)(2,1)S(1)} custom-call(bf16[12,512,1024]{2,1,0:T(8,128)(2,1)S(1)} %bitcast.24, bf16[12,512,128]{2,1,0:T(8,128)(2,1)S(1)} %bitcast.27, f32[128,1024]{1,0:T(8,128)S(1)} %copy-done.6, f32[128,1024]{1,0:T(8,128)S(1)} %copy-done.7, bf16[2304,8192]{1,0:T(8,128)(2,1)} %get-tuple-element.9.order_ref.refs_1_.refs_2_), custom_call_target="tpu_custom_call" | custom-call | flops 1610612736 | bytes 12582912 | tf_op jit(solution)/shard_map/steps_up/pallas_call | solution.py:230
  125.6 0.0 slice-start.2
  125.6 0.0 copy-start.3
  125.6 0.0 copy-start.5
  125.6 31.1 %project_up.1.order_ref.refs_3_ = f32[8,12,1024]{2,1,0:T(8,128)S(1)} custom-call(bf16[1536,1024]{1,0:T(8,128)(2,1)S(1)} %steps_up.1.refs_0_, bf16[2304,8192]{1,0:T(8,128)(2,1)} %get-tuple-element.9.order_ref.refs_1_.refs_2_, bf16[2304,8192]{1,0:T(8,128)(2,1)} %get-tuple-element.9.order_ref.refs_1_.refs_2_), custom_call_target="tpu_custom_call" | custom-call | flops 25769803776 | bytes 19922944 | tf_op jit(solution)/shard_map/project_up/pallas_call | solution.py:282
  156.7 0.0 slice-done
  156.7 0.0 slice-done.1
  156.7 0.0 slice-done.2
  156.7 0.0 copy-done.3
  156.7 0.0 copy-done.5
  156.8 4.9 %steps_down.1.refs_0_ = bf16[1536,1024]{1,0:T(8,128)(2,1)S(1)} custom-call(bf16[12,512,1024]{2,1,0:T(8,128)(2,1)S(1)} %bitcast.22, bf16[12,512,128]{2,1,0:T(8,128)(2,1)S(1)} %bitcast.28, f32[128,1024]{1,0:T(8,128)S(1)} %bitcast.25, f32[128,1024]{1,0:T(8,128)S(1)} %bitcast.26, f32[8,12,1024]{2,1,0:T(8,128)S(1)} %project_up.1.order_ref.refs_3_), custom_call_target="tpu_custom_call" | custom-call | flops 1610612736 | bytes 12582912 | tf_op jit(solution)/shard_map/steps_down/pallas_call | solution.py:230
  161.6 0.1 fusion.2.hot_ref
  161.7 0.0 copy-start.1
  161.7 31.1 %project_down.1.proj_ref = f32[8,12,1024]{2,1,0:T(8,128)S(1)} custom-call(bf16[1536,1024]{1,0:T(8,128)(2,1)S(1)} %steps_down.1.refs_0_, bf16[2304,8192]{1,0:T(8,128)(2,1)} %get-tuple-element.9.order_ref.refs_1_.refs_2_, bf16[2304,8192]{1,0:T(8,128)(2,1)} %get-tuple-element.9.order_ref.refs_1_.refs_2_, f32[8,12,1024]{2,1,0:T(8,128)S(1)} %project_up.1.order_ref.refs_3_), custom_call_target="tpu_custom_call" | custom-call | flops 25769803776 | bytes 19922944 | tf_op jit(solution)/shard_map/project_down/pallas_call | solution.py:282
  192.8 0.0 all-gather.2.cloned.1.call-done
  192.8 0.0 copy-start.2
  192.8 3.2 %multiply_reduce_fusion = f32[8,256]{1,0:T(8,128)S(1)} fusion(bf16[8,256,1024]{2,1,0:T(8,128)(2,1)} %all-gather.2.cloned.1.call-done), kind=kLoop, calls=%fused_computation | loop fusion | flops 6289408 | bytes 4202496 | tf_op jit(solution)/shard_map/reduce_sum | solution.py:450
  196.0 0.1 multiply_reduce_fusion.1.square_ref
  196.2 0.1 copy-done.2
  196.3 27.9 %finish.1 = (f32[12,1024]{1,0:T(8,128)S(1)}, f32[12,128]{1,0:T(8,128)S(1)}) custom-call(f32[8,12,1024]{2,1,0:T(8,128)S(1)} %project_down.1.proj_ref, bf16[2048,1024]{1,0:T(8,128)(2,1)S(1)} %bitcast.20, f32[12,8]{1,0:T(8,128)S(1)} %fusion.2.hot_ref, f32[12,256]{1,0:T(8,128)S(1)} %multiply_reduce_fusion.1.square_ref, s32[12,1]{1,0:T(8,128)S(1)} %copy.25.count_ref), custom_call_target="tpu_custom_call" | custom-call | tf_op jit(solution)/shard_map/finish/pallas_call | solution.py:371
  224.2 0.6 slice_reduce_fusion
  224.8 0.6 copy.28
  225.4 0.0 copy-done.1
  (3 shorter events, 0.0 us)
Async XLA Ops:
  7.2 1.4 copy-start
  7.2 185.6 %all-gather.2.cloned.1.call-start = ((), (), s32[]{:S(2)}) async-start(), calls=%async_computation | async-start | bytes 5242880 | tf_op jit(solution)/shard_map/all_gather | solution.py:448
  8.6 8.1 %copy-start.10 = (s32[12,1]{0,1:T(1,128)S(1)}, s32[12,1]{0,1:T(1,128)}, u32[]{:S(2)}) copy-start(s32[12,1]{0,1:T(1,128)} %param.21) | copy-start | bytes 148
  8.6 8.1 %copy-start.11 = (s32[8]{0:T(128)S(1)}, s32[8]{0:T(128)}, u32[]{:S(2)}) copy-start(s32[8]{0:T(128)} %param.22) | copy-start | bytes 100
  8.6 8.4 %copy-start.8 = (f32[1024,128]{1,0:T(8,128)S(1)}, f32[1024,128]{1,0:T(8,128)}, u32[]{:S(2)}) copy-start(f32[1024,128]{1,0:T(8,128)} %param.16) | copy-start | bytes 1572868
  8.6 8.6 %copy-start.9 = (f32[1024,128]{1,0:T(8,128)S(1)}, f32[1024,128]{1,0:T(8,128)}, u32[]{:S(2)}) copy-start(f32[1024,128]{1,0:T(8,128)} %param.17) | copy-start | bytes 1572868
  18.3 102.4 %slice-start.3 = ((s8[12582912]{0:T(1024)(128)(4,1)}), s8[4194304]{0:T(1024)(128)(4,1)S(1)}, s32[]{:S(2)}) async-start(s8[12582912]{0:T(1024)(128)(4,1)} %bitcast.23), calls=%async_computation.4 | async-start | bytes 8388608
  18.4 102.3 %slice-start.4 = ((s8[12582912]{0:T(1024)(128)(4,1)}), s8[4194304]{0:T(1024)(128)(4,1)S(1)}, s32[]{:S(2)}) async-start(s8[12582912]{0:T(1024)(128)(4,1)} %bitcast.23), calls=%async_computation.5 | async-start | bytes 8388608
  18.4 102.3 %slice-start.5 = ((s8[12582912]{0:T(1024)(128)(4,1)}), s8[4194304]{0:T(1024)(128)(4,1)S(1)}, s32[]{:S(2)}) async-start(s8[12582912]{0:T(1024)(128)(4,1)} %bitcast.23), calls=%async_computation.6 | async-start | bytes 8388608
  18.4 102.3 %copy-start.6 = (f32[128,1024]{1,0:T(8,128)S(1)}, f32[128,1024]{1,0:T(8,128)}, u32[]{:S(2)}) copy-start(f32[128,1024]{1,0:T(8,128)} %moment_ref.1) | copy-start | bytes 1572868
  18.4 102.3 %copy-start.7 = (f32[128,1024]{1,0:T(8,128)S(1)}, f32[128,1024]{1,0:T(8,128)}, u32[]{:S(2)}) copy-start(f32[128,1024]{1,0:T(8,128)} %second_ref.1) | copy-start | bytes 1572868
  119.5 1.2 copy-start.4
  120.7 36.0 %slice-start = ((s8[12582912]{0:T(1024)(128)(4,1)}), s8[4194304]{0:T(1024)(128)(4,1)S(1)}, s32[]{:S(2)}) async-start(s8[12582912]{0:T(1024)(128)(4,1)} %bitcast.21), calls=%async_computation.1 | async-start | bytes 8388608
  120.8 36.0 %slice-start.1 = ((s8[12582912]{0:T(1024)(128)(4,1)}), s8[4194304]{0:T(1024)(128)(4,1)S(1)}, s32[]{:S(2)}) async-start(s8[12582912]{0:T(1024)(128)(4,1)} %bitcast.21), calls=%async_computation.2 | async-start | bytes 8388608
  125.6 31.1 %slice-start.2 = ((s8[12582912]{0:T(1024)(128)(4,1)}), s8[4194304]{0:T(1024)(128)(4,1)S(1)}, s32[]{:S(2)}) async-start(s8[12582912]{0:T(1024)(128)(4,1)} %bitcast.21), calls=%async_computation.3 | async-start | bytes 8388608
  125.6 31.1 %copy-start.3 = (f32[1024,128]{0,1:T(8,128)S(1)}, f32[1024,128]{0,1:T(8,128)}, u32[]{:S(2)}) copy-start(f32[1024,128]{0,1:T(8,128)} %copy.24) | copy-start | bytes 1572868
  125.6 31.1 %copy-start.5 = (bf16[6144,128]{1,0:T(8,128)(2,1)S(1)}, bf16[6144,128]{1,0:T(8,128)(2,1)}, u32[]{:S(2)}) copy-start(bf16[6144,128]{1,0:T(8,128)(2,1)} %copy-done.4) | copy-start | bytes 4718596
  161.7 63.7 %copy-start.1 = (bf16[1024,128]{1,0:T(8,128)(2,1)S(1)}, bf16[1024,128]{1,0:T(8,128)(2,1)}, u32[]{:S(2)}) copy-start(bf16[1024,128]{1,0:T(8,128)(2,1)} %param.14) | copy-start | bytes 786436
  192.8 3.5 %copy-start.2 = (bf16[8,256,1024]{2,1,0:T(8,128)(2,1)S(1)}, bf16[8,256,1024]{2,1,0:T(8,128)(2,1)}, u32[]{:S(2)}) copy-start(bf16[8,256,1024]{2,1,0:T(8,128)(2,1)} %all-gather.2.cloned.1.call-done) | copy-start | bytes 12582916
Sparse Core Ops, SparseCore 0:
  9.6 37.1 all-gather.1
